TPU v7x, 768 devices: a whole 4x8x12 slice. The times are simulated.
768 devices in a mesh: dp: 64 (over y, x, core), pipe: 12 (over z).
Axes of the slice: x: 4, y: 8, z: 12, core: 2. Of those that a mesh axis runs over, the one named last changes fastest.
Arguments:
- queries: bfloat16 [12, 15360, 2560], P('pipe', 'dp'), may hold values from -6 to 6
- key_rows: bfloat16 [12, 15360, 512], P('pipe', 'dp'), may hold values from -6 to 6
- value_rows: bfloat16 [12, 15360, 512], P('pipe', 'dp'), may hold values from -6 to 6
- out_grad: bfloat16 [12, 15360, 2560], P('pipe', 'dp'), may hold values from -6 to 6
- log_norm: bfloat16 [12, 20, 15360], P('pipe', None, 'dp'), may hold values from 2.5 to 4.5
- row_delta: bfloat16 [12, 20, 15360], P('pipe', None, 'dp'), may hold values from -24 to 24
- cand_lengths: int32 [12, 64, 3], P('pipe', 'dp'), may hold values from 0 to 80, as said below
Outputs:
- up_q: bfloat16 [12, 15360, 2560], P('pipe', 'dp')
- up_k: bfloat16 [12, 15360, 512], P('pipe', 'dp')
- up_v: bfloat16 [12, 15360, 512], P('pipe', 'dp')
- bias_grad: float32 [12, 3072], P('pipe', 'dp')
- value_bias_grad: float32 [12, 512], P('pipe', 'dp')
Inputs may be any that keep to these rules, and one draw needn't show every extreme that they name: `cand_lengths`: each block's candidates fill its slots from the front, zeros marking empty slots, and the first slot is never empty; nonzero lengths are 64 or more, and the lengths of one block sum to at most 240. For the blocks i and i + 32 of one section, the rows of one block's candidates that end within its first 160 rows plus the rows of the other block's candidates that end beyond them come to at most 160, both ways round.
All inputs are finite; a program needn't handle non-finite values.
Results may differ from a plain program's by a relative error of at most 0.0054.
Values may be sent and summed in bfloat16 or wider, within the bound.
No kernel may reach another device: no remote copies, remote signals or barrier semaphores. Data moves between devices by JAX's collectives and lax.ppermute only.
A program may use at most 32 MiB of HBM per device.

v0:
```python
import math

import jax
import jax.numpy as jnp
from jax import lax
from jax.sharding import PartitionSpec as P

HEADS = 20
KV_HEADS = 4
HEAD_DIM = 128
HOME_ROWS = 240
BAL_ROWS = 160
MOVE_ROWS = 80


def passed_along(value, axis, steps):
    count = lax.axis_size(axis)
    pairs = [(source, (source + steps) % count) for source in range(count)]
    return lax.ppermute(value, axis, pairs)


def partner(value, axis, apart):
    mask = 2**apart
    pairs = [(source, source ^ mask) for source in range(lax.axis_size(axis))]
    return lax.ppermute(value, axis, pairs)


def segment_mask(lengths, row_count):
    row_ends = jnp.cumsum(lengths)
    position = jnp.arange(row_count, dtype=jnp.int32)
    labels = jnp.sum((position[:, None] >= row_ends[None, :]).astype(jnp.int32), axis=1)
    inside = position < row_ends[-1]
    return (labels[:, None] == labels[None, :]) & inside[:, None] & inside[None, :]


def pad_axis(tensor, extra_rows, dim_index):
    widths = [(0, 0)] * tensor.ndim
    widths[dim_index] = (0, extra_rows)
    return jnp.pad(tensor, widths)


def take_block(tensor, offset, dim_index):
    return lax.dynamic_slice_in_dim(
        pad_axis(tensor, MOVE_ROWS, dim_index), offset, MOVE_ROWS, dim_index
    )


def place_block(tensor, piece_rows, offset, dim_index, keep_count):
    padded = pad_axis(tensor, MOVE_ROWS, dim_index)
    placed = lax.dynamic_update_slice_in_dim(padded, piece_rows, offset, dim_index)
    return lax.slice_in_dim(placed, 0, keep_count, axis=dim_index)


def partner_bit():
    return lax.axis_size("dp").bit_length() - 2


def attend_backward(query_rows, key_part, value_part, grad_rows, norm_rows, delta_rows, allowed):
    row_count = query_rows.shape[0]
    per_group = HEADS // KV_HEADS
    factor = 1.0 / math.sqrt(HEAD_DIM)
    query_groups = jnp.moveaxis(query_rows.reshape(row_count, KV_HEADS, per_group * HEAD_DIM), 1, 0)
    grad_groups = jnp.moveaxis(grad_rows.reshape(row_count, KV_HEADS, per_group * HEAD_DIM), 1, 0)
    key_groups = jnp.moveaxis(key_part.reshape(row_count, KV_HEADS, HEAD_DIM), 1, 0)
    value_groups = jnp.moveaxis(value_part.reshape(row_count, KV_HEADS, HEAD_DIM), 1, 0)
    norm_groups = norm_rows.reshape(KV_HEADS, per_group, row_count)
    delta_groups = delta_rows.reshape(KV_HEADS, per_group, row_count)

    def one_group(pieces):
        query_part, key_group, value_group, grad_part, norm_part, delta_part = pieces
        query_heads = query_part.reshape(row_count, per_group, HEAD_DIM)
        grad_heads = grad_part.reshape(row_count, per_group, HEAD_DIM)
        scores = (
            jnp.einsum("igd,jd->gij", query_heads, key_group, preferred_element_type=jnp.float32)
            * factor
        )
        shifted = scores - norm_part.astype(jnp.float32)[:, :, None]
        probs = jnp.where(allowed[None], jnp.exp(shifted), 0.0)
        dprobs = jnp.einsum(
            "igd,jd->gij", grad_heads, value_group, preferred_element_type=jnp.float32
        )
        dscores = probs * (dprobs - delta_part.astype(jnp.float32)[:, :, None])
        probs_low = probs.astype(jnp.bfloat16)
        dscores_low = dscores.astype(jnp.bfloat16)
        grad_value = jnp.einsum(
            "gij,igd->jd", probs_low, grad_heads, preferred_element_type=jnp.float32
        )
        grad_key = (
            jnp.einsum("gij,igd->jd", dscores_low, query_heads, preferred_element_type=jnp.float32)
            * factor
        )
        grad_query = (
            jnp.einsum("gij,jd->igd", dscores_low, key_group, preferred_element_type=jnp.float32)
            * factor
        )
        return (
            grad_query.reshape(row_count, per_group * HEAD_DIM).astype(jnp.bfloat16),
            grad_key.astype(jnp.bfloat16),
            grad_value.astype(jnp.bfloat16),
        )

    grad_query, grad_key, grad_value = lax.map(
        one_group, (query_groups, key_groups, value_groups, grad_groups, norm_groups, delta_groups)
    )
    grad_query = jnp.moveaxis(grad_query, 0, 1).reshape(row_count, HEADS * HEAD_DIM)
    grad_key = jnp.moveaxis(grad_key, 0, 1).reshape(row_count, KV_HEADS * HEAD_DIM)
    grad_value = jnp.moveaxis(grad_value, 0, 1).reshape(row_count, KV_HEADS * HEAD_DIM)
    return (grad_query, grad_key, grad_value)


def send_up(gradients):
    return passed_along((gradients[0], gradients[1], gradients[2]), "pipe", -1)


def return_rows(gradients, kept_rows):
    bit_number = partner_bit()
    returned = partner(
        (
            take_block(gradients[0], kept_rows, 0),
            take_block(gradients[1], kept_rows, 0),
            take_block(gradients[2], kept_rows, 0),
        ),
        "dp",
        bit_number,
    )
    position = jnp.arange(BAL_ROWS, dtype=jnp.int32)
    own_rows = position[:, None] < kept_rows
    restored = []
    for index in range(3):
        masked = jnp.where(own_rows, gradients[index], jnp.zeros((), jnp.bfloat16))
        base_rows = pad_axis(masked, HOME_ROWS - BAL_ROWS, 0)
        restored.append(place_block(base_rows, returned[index], kept_rows, 0, HOME_ROWS))
    return (restored[0], restored[1], restored[2])


def column_totals(parts):
    ones_row = jnp.ones((1, HOME_ROWS), jnp.bfloat16)
    query_key = jnp.concatenate(
        [
            jnp.dot(ones_row, parts[0], preferred_element_type=jnp.float32)[0],
            jnp.dot(ones_row, parts[1], preferred_element_type=jnp.float32)[0],
        ]
    )
    value_part = jnp.dot(ones_row, parts[2], preferred_element_type=jnp.float32)[0]
    return (query_key, value_part)


def shards(queries, key_rows, value_rows, out_grad, log_norm, row_delta, cand_lengths):
    query_home = queries[0]
    key_home = key_rows[0]
    value_home = value_rows[0]
    grad_home = out_grad[0]
    norm_home = log_norm[0]
    delta_home = row_delta[0]
    lengths = cand_lengths[0, 0]
    row_ends = jnp.cumsum(lengths)
    kept_lengths = jnp.where(row_ends <= BAL_ROWS, lengths, 0)
    moved_lengths = lengths - kept_lengths
    kept_rows = jnp.sum(kept_lengths)
    bit_number = partner_bit()
    incoming = partner(
        (
            take_block(query_home, kept_rows, 0),
            take_block(key_home, kept_rows, 0),
            take_block(value_home, kept_rows, 0),
            take_block(grad_home, kept_rows, 0),
            take_block(norm_home, kept_rows, 1),
            take_block(delta_home, kept_rows, 1),
            moved_lengths.astype(jnp.bfloat16),
        ),
        "dp",
        bit_number,
    )

    def settle(tensor, piece_rows, dim_index):
        front = lax.slice_in_dim(tensor, 0, BAL_ROWS, axis=dim_index)
        return place_block(front, piece_rows, kept_rows, dim_index, BAL_ROWS)

    arrived = incoming[6].astype(jnp.int32)
    allowed = segment_mask(jnp.concatenate([kept_lengths, arrived]), BAL_ROWS)
    gradients = attend_backward(
        settle(query_home, incoming[0], 0),
        settle(key_home, incoming[1], 0),
        settle(value_home, incoming[2], 0),
        settle(grad_home, incoming[3], 0),
        settle(norm_home, incoming[4], 1),
        settle(delta_home, incoming[5], 1),
        allowed,
    )
    received = send_up(return_rows(gradients, kept_rows))
    query_key_sums, value_sums = column_totals(received)
    bias_grad, value_bias_grad = (
        lax.psum_scatter(query_key_sums, "dp", scatter_dimension=0, tiled=True),
        lax.psum_scatter(value_sums, "dp", scatter_dimension=0, tiled=True),
    )
    return (
        received[0][None],
        received[1][None],
        received[2][None],
        bias_grad[None],
        value_bias_grad[None],
    )


def solution(mesh):
    in_specs = (
        P("pipe", "dp", None),
        P("pipe", "dp", None),
        P("pipe", "dp", None),
        P("pipe", "dp", None),
        P("pipe", None, "dp"),
        P("pipe", None, "dp"),
        P("pipe", "dp", None),
    )
    out_specs = (
        P("pipe", "dp", None),
        P("pipe", "dp", None),
        P("pipe", "dp", None),
        P("pipe", "dp"),
        P("pipe", "dp"),
    )
    return jax.shard_map(shards, mesh=mesh, in_specs=in_specs, out_specs=out_specs, check_vma=False)
```

profile of v0, /device:TPU:448, one launch (start us, length us, event | category | flops | bytes accessed | tf_op | source)
XLA Modules:
  0.0 423.4 jit_solution(6599036279897564173)
XLA Ops:
  2.2 7.7 %collective-permute-start.1 = (bf16[3]{0:T(256)(128)(2,1)S(1)}, bf16[3]{0:T(256)(128)(2,1)S(1)}, u32[]{:S(2)}, u32[]{:S(2)}) collective-permute-start(bf16[3]{0:T(256)(128)(2,1)S(1)} %get-tuple-element.157), channel_id=1, source_target_pairs={{0,384},{12,396},{24,408},{36,420},{48,432},{60,444},{72,456},{84,... | collective-permute-start | bytes 26 | tf_op jit(solution)/shard_map/ppermute | solution.py:25
  13.3 2.0 collective-permute-start.3
  16.1 7.7 %collective-permute-start.6 = (bf16[20,80]{1,0:T(8,128)(2,1)S(1)}, bf16[20,80]{1,0:T(8,128)(2,1)S(1)}, u32[]{:S(2)}, u32[]{:S(2)}) collective-permute-start(bf16[20,80]{1,0:T(8,128)(2,1)S(1)} %pad_dynamic-slice_fusion.7), channel_id=1, source_target_pairs={{0,384},{12,396},{24,408},{36,420},{48,432},{60,444},{72,456},{84,... | collective-permute-start | bytes 9608 | tf_op jit(solution)/shard_map/ppermute | solution.py:25
  23.8 1.9 pad_dynamic-slice_fusion.1
  25.8 2.1 collective-permute-start.2
  28.8 7.7 %collective-permute-start.5 = (bf16[80,2560]{1,0:T(8,128)(2,1)}, bf16[80,2560]{1,0:T(8,128)(2,1)}, u32[]{:S(2)}, u32[]{:S(2)}) collective-permute-start(bf16[80,2560]{1,0:T(8,128)(2,1)} %pad_dynamic-slice_fusion), channel_id=1, source_target_pairs={{0,384},{12,396},{24,408},{36,420},{48,432},{60,444},{72,456},{84,... | collective-permute-start | bytes 1228808 | tf_op jit(solution)/shard_map/ppermute | solution.py:25
  41.7 2.0 collective-permute-start
  44.7 7.7 %collective-permute-start.4 = (bf16[80,512]{1,0:T(8,128)(2,1)}, bf16[80,512]{1,0:T(8,128)(2,1)}, u32[]{:S(2)}, u32[]{:S(2)}) collective-permute-start(bf16[80,512]{1,0:T(8,128)(2,1)} %pad_dynamic-slice_fusion.3), channel_id=1, source_target_pairs={{0,384},{12,396},{24,408},{36,420},{48,432},{60,444},{72,456},{84,... | collective-permute-start | bytes 245768 | tf_op jit(solution)/shard_map/ppermute | solution.py:25
  53.7 12.1 %collective-permute-done = bf16[80,512]{1,0:T(8,128)(2,1)S(1)} collective-permute-done((bf16[80,512]{1,0:T(8,128)(2,1)S(1)}, bf16[80,512]{1,0:T(8,128)(2,1)S(1)}, u32[]{:S(2)}, u32[]{:S(2)}) %collective-permute-start) | collective-permute-done | bytes 81952 | tf_op jit(solution)/shard_map/ppermute | solution.py:25
  66.5 9.5 %collective-permute-done.4 = bf16[80,512]{1,0:T(8,128)(2,1)} collective-permute-done((bf16[80,512]{1,0:T(8,128)(2,1)}, bf16[80,512]{1,0:T(8,128)(2,1)}, u32[]{:S(2)}, u32[]{:S(2)}) %collective-permute-start.4) | collective-permute-done | bytes 81952 | tf_op jit(solution)/shard_map/ppermute | solution.py:25
  75.9 1.3 dynamic_update_slice.41
  78.0 3.1 dynamic_update_slice.39
  81.5 3.1 dynamic_update_slice.42
  84.7 1.1 reshape.141
  85.8 1.3 copy.51
  87.1 16.6 %while.15 = (s32[]{:T(128)}, bf16[4,160,640]{2,1,0:T(8,128)(2,1)}, bf16[4,160,128]{2,1,0:T(8,128)(2,1)S(1)}, bf16[4,160,128]{2,1,0:T(8,128)(2,1)S(1)}, bf16[4,16...) while((s32[]{:T(128)}, bf16[4,160,640]{2,1,0:T(8,128)(2,1)}, ...), condition=%wide.region_5.6_spmd.clone, body=%wide.region_4.5_spmd.clone.sunk | while | flops 165080640 | bytes 7471557 | solution.py:102
  88.5 1.1 fusion.76
  96.7 1.1 fusion.76
  100.9 1.1 fusion.76
  103.7 1.2 copy.56
  105.0 1.9 collective-permute-start.11
  107.1 7.8 %collective-permute-start.7 = (bf16[80,2560]{1,0:T(8,128)(2,1)S(1)}, bf16[80,2560]{1,0:T(8,128)(2,1)S(1)}, u32[]{:S(2)}, u32[]{:S(2)}) collective-permute-start(bf16[80,2560]{1,0:T(8,128)(2,1)S(1)} %pad_dynamic-slice_fusion.2), channel_id=1, source_target_pairs={{0,384},{12,396},{24,408},{36,420},{48,432},{60,444},{72,456},{84,... | collective-permute-start | bytes 1228808 | tf_op jit(solution)/shard_map/ppermute | solution.py:25
  115.2 15.3 %collective-permute-done.7 = bf16[80,2560]{1,0:T(8,128)(2,1)S(1)} collective-permute-done((bf16[80,2560]{1,0:T(8,128)(2,1)S(1)}, bf16[80,2560]{1,0:T(8,128)(2,1)S(1)}, u32[]{:S(2)}, u32[]{:S(2)}) %collective-permute-start.7) | collective-permute-done | bytes 409632 | tf_op jit(solution)/shard_map/ppermute | solution.py:25
  130.5 2.1 dynamic_update_slice.44
  132.7 1.9 collective-permute-start.8
  134.7 7.1 %collective-permute-start.9 = (bf16[80,512]{1,0:T(8,128)(2,1)S(1)}, bf16[80,512]{1,0:T(8,128)(2,1)S(1)}, u32[]{:S(2)}, u32[]{:S(2)}) collective-permute-start(bf16[80,512]{1,0:T(8,128)(2,1)S(1)} %pad_dynamic-slice_fusion.6), channel_id=1, source_target_pairs={{0,384},{12,396},{24,408},{36,420},{48,432},{60,444},{72,456},{84,... | collective-permute-start | bytes 245768 | tf_op jit(solution)/shard_map/ppermute | solution.py:25
  142.8 1.9 collective-permute-start.12
  146.4 1.9 collective-permute-start.10
  148.3 1.3 dynamic-slice
  150.9 4.3 %collective-permute-done.12 = bf16[240,512]{1,0:T(8,128)(2,1)S(1)} collective-permute-done((bf16[240,512]{1,0:T(8,128)(2,1)S(1)}, bf16[240,512]{1,0:T(8,128)(2,1)S(1)}, u32[]{:S(2)}, u32[]{:S(2)}) %collective-permute-start.12) | collective-permute-done | bytes 245792 | tf_op jit(solution)/shard_map/ppermute | solution.py:19
  155.1 2.6 collective-permute-done.10
  158.3 261.5 %all-reduce.21 = (f32[3072]{0:T(1024)S(1)}, f32[512]{0:T(512)S(1)}) all-reduce(f32[3072]{0:T(1024)S(1)} %pad_maximum_fusion, f32[512]{0:T(512)S(1)} %bitcast.177), channel_id=2, replica_groups=mesh['dp'=64,'pipe'=12] {'dp'}, use_global_device_ids=true, to_apply=%region_6.7.clone | all-reduce | flops 3584 | bytes 28672
  (143 shorter events, 32.7 us)
Async XLA Ops:
  0.6 27.3 %copy-start.1 = (bf16[1,240,2560]{2,1,0:T(8,128)(2,1)S(1)}, bf16[1,240,2560]{2,1,0:T(8,128)(2,1)}, u32[]{:S(2)}) copy-start(bf16[1,240,2560]{2,1,0:T(8,128)(2,1)} %param.12) | copy-start | bytes 3686404
  2.2 39.5 %collective-permute-start.1 = (bf16[3]{0:T(256)(128)(2,1)S(1)}, bf16[3]{0:T(256)(128)(2,1)S(1)}, u32[]{:S(2)}, u32[]{:S(2)}) collective-permute-start(bf16[3]{0:T(256)(128)(2,1)S(1)} %get-tuple-element.157), channel_id=1, source_target_pairs={{0,384},{12,396},{24,408},{36,420},{48,432},{60,444},{72,456},{84,... | collective-permute-start | bytes 26 | tf_op jit(solution)/shard_map/ppermute | solution.py:25
  13.3 40.1 %collective-permute-start.3 = (bf16[20,80]{1,0:T(8,128)(2,1)S(1)}, bf16[20,80]{1,0:T(8,128)(2,1)S(1)}, u32[]{:S(2)}, u32[]{:S(2)}) collective-permute-start(bf16[20,80]{1,0:T(8,128)(2,1)S(1)} %pad_dynamic-slice_fusion.8), channel_id=1, source_target_pairs={{0,384},{12,396},{24,408},{36,420},{48,432},{60,444},{72,456},{84,... | collective-permute-start | bytes 9608 | tf_op jit(solution)/shard_map/ppermute | solution.py:25
  16.1 28.5 %collective-permute-start.6 = (bf16[20,80]{1,0:T(8,128)(2,1)S(1)}, bf16[20,80]{1,0:T(8,128)(2,1)S(1)}, u32[]{:S(2)}, u32[]{:S(2)}) collective-permute-start(bf16[20,80]{1,0:T(8,128)(2,1)S(1)} %pad_dynamic-slice_fusion.7), channel_id=1, source_target_pairs={{0,384},{12,396},{24,408},{36,420},{48,432},{60,444},{72,456},{84,... | collective-permute-start | bytes 9608 | tf_op jit(solution)/shard_map/ppermute | solution.py:25
  25.8 10.8 %copy-start = (bf16[1,240,2560]{2,1,0:T(8,128)(2,1)S(1)}, bf16[1,240,2560]{2,1,0:T(8,128)(2,1)}, u32[]{:S(2)}) copy-start(bf16[1,240,2560]{2,1,0:T(8,128)(2,1)} %param.9) | copy-start | bytes 3686404
  25.8 52.2 %collective-permute-start.2 = (bf16[80,2560]{1,0:T(8,128)(2,1)}, bf16[80,2560]{1,0:T(8,128)(2,1)}, u32[]{:S(2)}, u32[]{:S(2)}) collective-permute-start(bf16[80,2560]{1,0:T(8,128)(2,1)} %pad_dynamic-slice_fusion.1), channel_id=1, source_target_pairs={{0,384},{12,396},{24,408},{36,420},{48,432},{60,444},{72,456},{84,... | collective-permute-start | bytes 1228808 | tf_op jit(solution)/shard_map/ppermute | solution.py:25
  28.8 52.7 %collective-permute-start.5 = (bf16[80,2560]{1,0:T(8,128)(2,1)}, bf16[80,2560]{1,0:T(8,128)(2,1)}, u32[]{:S(2)}, u32[]{:S(2)}) collective-permute-start(bf16[80,2560]{1,0:T(8,128)(2,1)} %pad_dynamic-slice_fusion), channel_id=1, source_target_pairs={{0,384},{12,396},{24,408},{36,420},{48,432},{60,444},{72,456},{84,... | collective-permute-start | bytes 1228808 | tf_op jit(solution)/shard_map/ppermute | solution.py:25
  36.6 2.3 copy-start.7
  36.6 2.3 copy-start.8
  36.7 2.3 copy-start.9
  36.7 2.3 copy-start.3
  36.7 3.0 copy-start.4
  39.8 1.1 copy-start.2
  41.7 24.2 %collective-permute-start = (bf16[80,512]{1,0:T(8,128)(2,1)S(1)}, bf16[80,512]{1,0:T(8,128)(2,1)S(1)}, u32[]{:S(2)}, u32[]{:S(2)}) collective-permute-start(bf16[80,512]{1,0:T(8,128)(2,1)S(1)} %pad_dynamic-slice_fusion.4), channel_id=1, source_target_pairs={{0,384},{12,396},{24,408},{36,420},{48,432},{60,444},{72,456},{84,... | collective-permute-start | bytes 245768 | tf_op jit(solution)/shard_map/ppermute | solution.py:25
  44.7 31.2 %collective-permute-start.4 = (bf16[80,512]{1,0:T(8,128)(2,1)}, bf16[80,512]{1,0:T(8,128)(2,1)}, u32[]{:S(2)}, u32[]{:S(2)}) collective-permute-start(bf16[80,512]{1,0:T(8,128)(2,1)} %pad_dynamic-slice_fusion.3), channel_id=1, source_target_pairs={{0,384},{12,396},{24,408},{36,420},{48,432},{60,444},{72,456},{84,... | collective-permute-start | bytes 245768 | tf_op jit(solution)/shard_map/ppermute | solution.py:25
  85.8 1.3 copy-start.5
  85.8 1.3 copy-start.6
  105.0 37.0 %collective-permute-start.11 = (bf16[80,512]{1,0:T(8,128)(2,1)S(1)}, bf16[80,512]{1,0:T(8,128)(2,1)S(1)}, u32[]{:S(2)}, u32[]{:S(2)}) collective-permute-start(bf16[80,512]{1,0:T(8,128)(2,1)S(1)} %pad_dynamic-slice_fusion.5), channel_id=1, source_target_pairs={{0,384},{12,396},{24,408},{36,420},{48,432},{60,444},{72,456},{84,... | collective-permute-start | bytes 245768 | tf_op jit(solution)/shard_map/ppermute | solution.py:25
  107.1 23.4 %collective-permute-start.7 = (bf16[80,2560]{1,0:T(8,128)(2,1)S(1)}, bf16[80,2560]{1,0:T(8,128)(2,1)S(1)}, u32[]{:S(2)}, u32[]{:S(2)}) collective-permute-start(bf16[80,2560]{1,0:T(8,128)(2,1)S(1)} %pad_dynamic-slice_fusion.2), channel_id=1, source_target_pairs={{0,384},{12,396},{24,408},{36,420},{48,432},{60,444},{72,456},{84,... | collective-permute-start | bytes 1228808 | tf_op jit(solution)/shard_map/ppermute | solution.py:25
  132.7 25.4 %collective-permute-start.8 = (bf16[240,2560]{1,0:T(8,128)(2,1)S(1)}, bf16[240,2560]{1,0:T(8,128)(2,1)S(1)}, u32[]{:S(2)}, u32[]{:S(2)}) collective-permute-start(bf16[240,2560]{1,0:T(8,128)(2,1)S(1)} %slice.83), channel_id=1, source_target_pairs={{0,11},{1,0},{2,1},{3,2},{4,3},{5,4},{6,5},{7,6},{8,7},{9,8},{10,9... | collective-permute-start | bytes 3686408 | tf_op jit(solution)/shard_map/ppermute | solution.py:19
  134.7 10.2 %collective-permute-start.9 = (bf16[80,512]{1,0:T(8,128)(2,1)S(1)}, bf16[80,512]{1,0:T(8,128)(2,1)S(1)}, u32[]{:S(2)}, u32[]{:S(2)}) collective-permute-start(bf16[80,512]{1,0:T(8,128)(2,1)S(1)} %pad_dynamic-slice_fusion.6), channel_id=1, source_target_pairs={{0,384},{12,396},{24,408},{36,420},{48,432},{60,444},{72,456},{84,... | collective-permute-start | bytes 245768 | tf_op jit(solution)/shard_map/ppermute | solution.py:25
  142.8 12.4 %collective-permute-start.12 = (bf16[240,512]{1,0:T(8,128)(2,1)S(1)}, bf16[240,512]{1,0:T(8,128)(2,1)S(1)}, u32[]{:S(2)}, u32[]{:S(2)}) collective-permute-start(bf16[240,512]{1,0:T(8,128)(2,1)S(1)} %slice.85), channel_id=1, source_target_pairs={{0,11},{1,0},{2,1},{3,2},{4,3},{5,4},{6,5},{7,6},{8,7},{9,8},{10,9... | collective-permute-start | bytes 737288 | tf_op jit(solution)/shard_map/ppermute | solution.py:19
  146.4 11.4 %collective-permute-start.10 = (bf16[240,512]{1,0:T(8,128)(2,1)}, bf16[240,512]{1,0:T(8,128)(2,1)S(1)}, u32[]{:S(2)}, u32[]{:S(2)}) collective-permute-start(bf16[240,512]{1,0:T(8,128)(2,1)} %slice.84), channel_id=1, source_target_pairs={{0,11},{1,0},{2,1},{3,2},{4,3},{5,4},{6,5},{7,6},{8,7},{9,8},{10,9... | collective-permute-start | bytes 737288 | tf_op jit(solution)/shard_map/ppermute | solution.py:19
where the time goes:
time: 425 us; the launch traced here: 423 us
  blocking collectives  261 us (61%)
  starting transfers between devices  59.7 us (14%)
  waiting for transfers between devices  44 us (10%)
  local copies, waits for them, and re-layouts  37.6 us (9%)
  matrix products  9.95 us (2%)
  between operations  5.79 us (1%)
  other arithmetic  4.6 us (1%)
    unnamed x1, blocking collectives  261 us
    ppermute x10, starting transfers between devices, partner(): return lax.ppermute(value, axis, pairs)  53.9 us
    ppermute x10, waiting for transfers between devices, partner(): return lax.ppermute(value, axis, pairs)  37.2 us
    dynamic_update_slice x9, local copies, waits for them, and re-layouts, place_block(): lax.dynamic_update_slice_in_dim(padded, piece_rows, offset, dim_index)  12.2 us
  transfers between devices with their start and end apart: 13, of which 6 were waited for; matrix products, arithmetic and copies ran while one was open for 5% of the time, Pallas kernels for 0%

commit v1 on v0

v1 whole, which is shorter than its diff:
```python
import functools
import math

import jax
import jax.numpy as jnp
from jax import lax
from jax.experimental import pallas as pl
from jax.experimental.pallas import tpu as pltpu
from jax.sharding import PartitionSpec as P


HEADS = 20
KV_HEADS = 4
HEAD_DIM = 128
PER_GROUP = HEADS // KV_HEADS
CANDIDATES = 3
LONGEST = 80
HOME_ROWS = 240
PAIR = 2
WIDTH = PER_GROUP * LONGEST
MAIN = WIDTH // 128 * 128
REST = WIDTH - MAIN
CORNER = 256
CHUNK = HOME_ROWS + REST
FACTOR = 1.0 / math.sqrt(HEAD_DIM)
BF16 = jnp.bfloat16
F32 = jnp.float32


def dot(left, right, left_dim=1, right_dim=0):
    return lax.dot_general(
        left, right, (((left_dim,), (right_dim,)), ((), ())), preferred_element_type=F32
    )


def iota(shape, axis):
    return lax.broadcasted_iota(jnp.int32, shape, axis)


def spans(lengths):
    starts = [jnp.zeros_like(lengths[0])]
    for c in range(CANDIDATES - 1):
        starts.append(starts[-1] + lengths[c])
    return starts, lengths


def stored_spans(lengths_ref):
    return spans([lengths_ref[0, c] for c in range(CANDIDATES)])


def sent_spans(ds_ref):
    corner = ds_ref[HOME_ROWS:CHUNK, CORNER:].astype(F32).astype(jnp.int32)
    return spans([corner[c : c + 1, :1] for c in range(CANDIDATES)])


def one_hot(hit):
    return jnp.where(hit, 1.0, 0.0).astype(BF16)


def to_slots(found):
    starts, lengths = found
    shape = (LONGEST, HOME_ROWS)
    row, home = iota(shape, 0), iota(shape, 1)
    return jnp.concatenate(
        [one_hot((home == row + starts[c]) & (row < lengths[c])) for c in range(CANDIDATES)], axis=0
    )


def to_home(found):
    starts, lengths = found
    shape = (HOME_ROWS, HOME_ROWS)
    home, slot = iota(shape, 0), iota(shape, 1)
    hit = jnp.zeros(shape, jnp.bool_)
    for c in range(CANDIDATES):
        j = slot - c * LONGEST
        hit = hit | ((home == j + starts[c]) & (j >= 0) & (j < lengths[c]))
    return one_hot(hit)


def rows_of(tensor, c):
    return tensor[c * LONGEST : (c + 1) * LONGEST]


def stacked(tensor, g, c):
    part = rows_of(tensor, c)
    base = g * PER_GROUP
    return jnp.concatenate(
        [part[:, (base + h) * HEAD_DIM : (base + h + 1) * HEAD_DIM] for h in range(PER_GROUP)], axis=0
    )


def scores_kernel(
    pair, lengths_ref, q_ref, k_ref, v_ref, o_ref, norm_ref, delta_ref, *refs
):
    ds_ref, dkv_ref = refs[-2:]
    found = stored_spans(lengths_ref)
    slots, home = to_slots(found), to_home(found)
    q = dot(slots, q_ref[...]).astype(BF16)
    k = dot(slots, k_ref[...]).astype(BF16)
    v = dot(slots, v_ref[...]).astype(BF16)
    o = dot(slots, o_ref[...]).astype(BF16)
    starts, lengths = found
    shape = (HOME_ROWS, WIDTH)
    at, lane = iota(shape, 0), iota(shape, 1)
    head_of = iota((PER_GROUP, WIDTH), 1)
    own = (head_of >= iota((PER_GROUP, WIDTH), 0) * LONGEST) & (
        head_of < (iota((PER_GROUP, WIDTH), 0) + 1) * LONGEST
    )
    within = lane
    for h in range(1, PER_GROUP):
        within = jnp.where(lane >= h * LONGEST, lane - h * LONGEST, within)
    rest = [[] for _ in range(PAIR)]
    dk = [[] for _ in range(PAIR)]
    dv = [[] for _ in range(PAIR)]
    for c in range(CANDIDATES):
        spread = one_hot((at == within + starts[c]) & (within < lengths[c]))
        norms = dot(norm_ref[...], spread)
        deltas = dot(delta_ref[...], spread)
        for g in range(PAIR):
            base = (pair * PAIR + g) * PER_GROUP
            norm = jnp.sum(jnp.where(own, norms[base : base + PER_GROUP], 0.0), axis=0, keepdims=True)
            delta = jnp.sum(jnp.where(own, deltas[base : base + PER_GROUP], 0.0), axis=0, keepdims=True)
            q_rows, o_rows = stacked(q, g, c), stacked(o, g, c)
            k_part = rows_of(k, c)[:, g * HEAD_DIM : (g + 1) * HEAD_DIM]
            v_part = rows_of(v, c)[:, g * HEAD_DIM : (g + 1) * HEAD_DIM]
            probs = jnp.exp(dot(k_part, q_rows, 1, 1) * FACTOR - norm)
            dscores = probs * (dot(v_part, o_rows, 1, 1) - delta)
            probs_low, dscores_low = probs.astype(BF16), dscores.astype(BF16)
            dk[g].append(dot(dscores_low, q_rows) * FACTOR)
            dv[g].append(dot(probs_low, o_rows))
            ds_ref[g * CHUNK + c * LONGEST : g * CHUNK + (c + 1) * LONGEST, :] = dscores_low[:, :MAIN]
            rest[g].append(dscores[:, MAIN:])
    for g in range(PAIR):
        for at, grads in ((g, dk[g]), (PAIR + g, dv[g])):
            rows = jnp.concatenate(grads, axis=0).astype(BF16)
            dkv_ref[:, at * HEAD_DIM : (at + 1) * HEAD_DIM] = dot(home, rows).astype(BF16)
        turned = jnp.concatenate(rest[g], axis=0).T
        tail = slice(g * CHUNK + HOME_ROWS, (g + 1) * CHUNK)
        ds_ref[tail, :CORNER] = jnp.zeros((REST, CORNER), BF16)
        ds_ref[tail, :HOME_ROWS] = turned.astype(BF16)
        corner = jnp.zeros((REST, MAIN - CORNER), F32)
        for c in range(CANDIDATES):
            corner = jnp.where(iota(corner.shape, 0) == c, lengths[c].astype(F32), corner)
        ds_ref[tail, CORNER:] = corner.astype(BF16)


def query_grads(ds_ref, k, g):
    k_group = k[:, g * HEAD_DIM : (g + 1) * HEAD_DIM]
    turned = ds_ref[g * CHUNK + HOME_ROWS : (g + 1) * CHUNK, :HOME_ROWS]
    lane = iota((REST, HOME_ROWS), 1)
    found = []
    for c in range(CANDIDATES):
        main = dot(
            ds_ref[g * CHUNK + c * LONGEST : g * CHUNK + (c + 1) * LONGEST, :], rows_of(k_group, c), 0, 0
        )
        mine = (lane >= c * LONGEST) & (lane < (c + 1) * LONGEST)
        last = dot(jnp.where(mine, turned.astype(F32), 0.0).astype(BF16), k_group)
        rows = (jnp.concatenate([main, last], axis=0) * FACTOR).astype(BF16)
        found.append(
            jnp.concatenate([rows[h * LONGEST : (h + 1) * LONGEST] for h in range(PER_GROUP)], axis=1)
        )
    return jnp.concatenate(found, axis=0)


def queries_kernel(k_ref, first_ref, second_ref, out_ref):
    found = sent_spans(first_ref)
    k = dot(to_slots(found), k_ref[...]).astype(BF16)
    home = to_home(found)
    width = PER_GROUP * HEAD_DIM
    for pair, ds_ref in enumerate((first_ref, second_ref)):

        @pl.when(pl.program_id(0) == pair)
        def _(ds_ref=ds_ref):
            for g in range(PAIR):
                out_ref[:, g * width : (g + 1) * width] = dot(home, query_grads(ds_ref, k, g)).astype(BF16)


def sums_kernel(lengths_ref, k_ref, first_ref, second_ref, dkv_ref, out_ref):
    k = dot(to_slots(stored_spans(lengths_ref)), k_ref[...]).astype(BF16)
    ranks = out_ref.shape[0] * out_ref.shape[1]

    def total(rows):
        return jnp.sum(rows.astype(F32), axis=0, keepdims=True)

    sums = []
    for pair, ds_ref in enumerate((first_ref, second_ref)):
        part = k[:, pair * PAIR * HEAD_DIM : (pair + 1) * PAIR * HEAD_DIM]
        sums += [total(query_grads(ds_ref, part, g)) for g in range(PAIR)]
    both = total(dkv_ref[...])
    parts = [both[:, at * KW : (at + 1) * KW] for at in range(2 * KV_HEADS // PAIR)]
    sums = jnp.concatenate(sums + parts[0::2], axis=1)
    value_sums = jnp.concatenate(parts[1::2], axis=1)
    step, value_step = sums.shape[1] // ranks, value_sums.shape[1] // ranks

    def folded(row, width):
        return jnp.concatenate([row[:, i * width : (i + 1) * width] for i in range(8)], axis=0)

    sums = folded(sums, 8 * step)
    pad = jnp.zeros((8, 128 - 8 * value_step), F32)
    value_sums = jnp.concatenate([folded(value_sums, 8 * value_step), pad], axis=1)
    lane = iota((8, 128), 1)
    for p in range(8):
        left = pltpu.roll(sums, (sums.shape[1] - step * p) % sums.shape[1], 1)[:, :128]
        right = pltpu.roll(value_sums, (step - value_step * p) % 128, 1)
        out_ref[:, p, :] = jnp.where(
            lane < step, left, jnp.where(lane < step + value_step, right, 0.0)
        )


def last_kernel(dkv_ref, sums_ref, k_ref, v_ref, bias_ref, value_bias_ref):
    for pair in range(KV_HEADS // PAIR):
        k_ref[:, pair * KW : (pair + 1) * KW] = dkv_ref[:, 2 * pair * KW : (2 * pair + 1) * KW]
        v_ref[:, pair * KW : (pair + 1) * KW] = dkv_ref[:, (2 * pair + 1) * KW : (2 * pair + 2) * KW]
    step = bias_ref.shape[1]
    bias_ref[...] = sums_ref[:, :step]
    value_bias_ref[...] = sums_ref[:, step : step + value_bias_ref.shape[1]]


VMEM_LIMIT = 67_043_328
SMEM = pl.BlockSpec(memory_space=pltpu.SMEM)


def whole(shape):
    return pl.BlockSpec(shape, lambda i: (0,) * len(shape))


def columns(width, at):
    return pl.BlockSpec((HOME_ROWS, width), lambda i: (0, at))


QW = PAIR * PER_GROUP * HEAD_DIM
KW = PAIR * HEAD_DIM


def kernel(body, flops, moved, exps=0, steps=1, **rest):
    return pl.pallas_call(
        body,
        grid=(steps,),
        cost_estimate=pl.CostEstimate(flops=flops, bytes_accessed=moved, transcendentals=exps),
        compiler_params=pltpu.CompilerParams(vmem_limit_bytes=VMEM_LIMIT),
        **rest,
    )


def score_grads(pair, lengths, q, k, v, o, norm, delta, earlier):
    shape = jax.ShapeDtypeStruct
    extra = () if earlier is None else (earlier,)
    return kernel(
        functools.partial(scores_kernel, pair),
        800_000_000,
        2_400_000,
        400_000,
        out_shape=(shape((PAIR * CHUNK, MAIN), BF16), shape((HOME_ROWS, 2 * KV_HEADS * HEAD_DIM), BF16)),
        in_specs=[
            SMEM,
            columns(QW, pair),
            columns(KW, pair),
            columns(KW, pair),
            columns(QW, pair),
            whole((HEADS, HOME_ROWS)),
            whole((HEADS, HOME_ROWS)),
        ]
        + [pl.BlockSpec(memory_space=pl.ANY)] * len(extra),
        out_specs=(whole((PAIR * CHUNK, MAIN)), columns(2 * KW, pair)),
        input_output_aliases={7: 1} if extra else {},
    )(lengths, q, k, v, o, norm, delta, *extra)


def query_out(k, ds):
    return kernel(
        queries_kernel,
        600_000_000,
        2_400_000,
        steps=KV_HEADS // PAIR,
        out_shape=jax.ShapeDtypeStruct((HOME_ROWS, HEADS * HEAD_DIM), BF16),
        in_specs=[pl.BlockSpec((HOME_ROWS, KW), lambda i: (0, i))] + [whole((PAIR * CHUNK, MAIN))] * 2,
        out_specs=pl.BlockSpec((HOME_ROWS, QW), lambda i: (0, i)),
    )(k, *ds)


def column_sums(ranks, lengths, k, ds, dkv):
    return kernel(
        sums_kernel,
        300_000_000,
        2_000_000,
        out_shape=jax.ShapeDtypeStruct((8, ranks // 8, 128), F32),
        in_specs=[SMEM, whole((HOME_ROWS, KV_HEADS * HEAD_DIM))]
        + [whole((PAIR * CHUNK, MAIN))] * 2
        + [whole((HOME_ROWS, 2 * KV_HEADS * HEAD_DIM))],
        out_specs=whole((8, ranks // 8, 128)),
    )(lengths, k, *ds, dkv)


def arrived(ranks, dkv, sums):
    shape = jax.ShapeDtypeStruct
    wide = KV_HEADS * HEAD_DIM
    small = ((HEADS + KV_HEADS) * HEAD_DIM // ranks, wide // ranks)
    return kernel(
        last_kernel,
        0,
        1_000_000,
        out_shape=(shape((HOME_ROWS, wide), BF16),) * 2 + tuple(shape((1, n), F32) for n in small),
        in_specs=[whole((HOME_ROWS, 2 * wide)), whole((1, 128))],
        out_specs=(whole((HOME_ROWS, wide)),) * 2 + tuple(whole((1, n)) for n in small),
    )(dkv, sums)


def up(value):
    count = lax.axis_size("pipe")
    return lax.ppermute(value, "pipe", [(s, (s - 1) % count) for s in range(count)])


def relay(q, k, v, o, norm, delta, lengths):
    ranks = lax.axis_size("dp")
    k_up = up(k)
    ds, ds_up, dkv = [], [], None
    for pair in range(KV_HEADS // PAIR):
        found, dkv = score_grads(pair, lengths, q, k, v, o, norm, delta, dkv)
        ds.append(found)
        ds_up.append(up(found))
    dkv_up = up(dkv)
    pieces = column_sums(ranks, lengths, k, ds, dkv)
    spread = lax.all_to_all(pieces.reshape(ranks, 1, 128), "dp", 0, 0, tiled=True)
    sums = up(jnp.sum(spread, axis=0))
    up_q = query_out(k_up, ds_up)
    return (up_q, *arrived(ranks, dkv_up, sums))


def shards(queries, key_rows, value_rows, out_grad, log_norm, row_delta, cand_lengths):
    up_q, up_k, up_v, bias, value_bias = relay(
        queries[0], key_rows[0], value_rows[0], out_grad[0], log_norm[0], row_delta[0], cand_lengths[0]
    )
    return up_q[None], up_k[None], up_v[None], bias, value_bias


def solution(mesh):
    in_specs = (
        P("pipe", "dp", None),
        P("pipe", "dp", None),
        P("pipe", "dp", None),
        P("pipe", "dp", None),
        P("pipe", None, "dp"),
        P("pipe", None, "dp"),
        P("pipe", "dp", None),
    )
    out_specs = (
        P("pipe", "dp", None),
        P("pipe", "dp", None),
        P("pipe", "dp", None),
        P("pipe", "dp"),
        P("pipe", "dp"),
    )
    return jax.shard_map(shards, mesh=mesh, in_specs=in_specs, out_specs=out_specs, check_vma=False)
```

time: 425 us -> 66.1 us (0.16)
  the two profiles are of different devices: /device:TPU:448 before, /device:TPU:1 now
where the time goes in v1:
time: 66.1 us; the launch traced here: 65.6 us
  starting transfers between devices  25 us (38%)
  blocking collectives  21.2 us (32%)
  Pallas kernels  18.1 us (27%)
  between operations  0.7 us (1%)
    ppermute x5, starting transfers between devices, up(): lax.ppermute(value, 'pipe', [(s, (s - 1) % count) for s in range(count)])  25 us
    all_to_all x1, blocking collectives, relay(): lax.all_to_all(pieces.reshape(ranks, 1, 128), 'dp', 0, 0, tiled=True)  21.2 us
    pallas_call x2, Pallas kernels, score_grads(): kernel(functools.partial(scores_kernel, pair), 800000000, 2400000, 400000...  8.93 us
    pallas_call x1, Pallas kernels, query_out(): kernel(queries_kernel, 600000000, 2400000, steps=KV_HEADS // PAIR, out_sh...  4.42 us
    pallas_call x1, Pallas kernels, column_sums(): kernel(sums_kernel, 300000000, 2000000, out_shape=jax.ShapeDtypeStruct((8...  2.88 us
    pallas_call x1, Pallas kernels, arrived(): kernel(last_kernel, 0, 1000000, out_shape=(shape((HOME_ROWS, wide), BF16)...  1.83 us
  transfers between devices with their start and end apart: 5, of which 0 were waited for; matrix products, arithmetic and copies ran while one was open for 1% of the time, Pallas kernels for 11%

profile of v1, /device:TPU:1, one launch (start us, length us, event | category | flops | bytes accessed | tf_op | source)
XLA Modules:
  0.0 65.6 jit_solution(34095833068447340)
XLA Ops:
  0.6 4.5 %shard_map.110 = (bf16[512,384]{1,0:T(8,128)(2,1)}, bf16[240,1024]{1,0:T(8,128)(2,1)}) custom-call(s32[1,3]{1,0:T(1,128)} %bitcast.30, bf16[240,2560]{1,0:T(8,128)(2,1)} %bitcast.14, bf16[240,512]{1,0:T(8,128)(2,1)} %bitcast.18, bf16[240,512]{1,0:T(8,128)(2,1)} %bitcast.23, bf16[240,2560]{1,0:T(8,128)(2,1)} %bitcast.16, bf16[20,240]{1,0:T(8,128)(2,1)} %bitcast.26, ...), custom_call_target="tpu_custom_call" | custom-call | flops 800000000 | bytes 2400000 | tf_op jit(solution)/shard_map/pallas_call | solution.py:248
  5.1 4.5 %shard_map.111 = (bf16[512,384]{1,0:T(8,128)(2,1)}, bf16[240,1024]{1,0:T(8,128)(2,1)}) custom-call(s32[1,3]{1,0:T(1,128)} %bitcast.31, bf16[240,2560]{1,0:T(8,128)(2,1)} %bitcast.15, bf16[240,512]{1,0:T(8,128)(2,1)} %bitcast.19, bf16[240,512]{1,0:T(8,128)(2,1)} %bitcast.24, bf16[240,2560]{1,0:T(8,128)(2,1)} %bitcast.17, ...), custom_call_target="tpu_custom_call", output_to_operand_aliasing={{1}: (7, {})} | custom-call | flops 800000000 | bytes 2400000 | tf_op jit(solution)/shard_map/pallas_call | solution.py:248
  9.6 15.1 %collective-permute-start.3 = (bf16[240,1024]{1,0:T(8,128)(2,1)}, bf16[240,1024]{1,0:T(8,128)(2,1)}, u32[]{:S(2)}, u32[]{:S(2)}) collective-permute-start(bf16[240,1024]{1,0:T(8,128)(2,1)} %get-tuple-element.16.dkv_ref), channel_id=1, source_target_pairs={{0,11},{1,0},{2,1},{3,2},{4,3},{5,4},{6,5},{7,6},{8,7},{9,8},{10,9... | collective-permute-start | bytes 1474568 | tf_op jit(solution)/shard_map/ppermute | solution.py:310
  24.7 2.2 %collective-permute-start.2 = (bf16[512,384]{1,0:T(8,128)(2,1)}, bf16[512,384]{1,0:T(8,128)(2,1)}, u32[]{:S(2)}, u32[]{:S(2)}) collective-permute-start(bf16[512,384]{1,0:T(8,128)(2,1)} %get-tuple-element.15.second_ref), channel_id=1, source_target_pairs={{0,11},{1,0},{2,1},{3,2},{4,3},{5,4},{6,5},{7,6},{8,7},{9,8},{10,9... | collective-permute-start | bytes 1179656 | tf_op jit(solution)/shard_map/ppermute | solution.py:310
  26.9 2.2 %collective-permute-start.1 = (bf16[512,384]{1,0:T(8,128)(2,1)}, bf16[512,384]{1,0:T(8,128)(2,1)}, u32[]{:S(2)}, u32[]{:S(2)}) collective-permute-start(bf16[512,384]{1,0:T(8,128)(2,1)} %get-tuple-element.13.first_ref), channel_id=1, source_target_pairs={{0,11},{1,0},{2,1},{3,2},{4,3},{5,4},{6,5},{7,6},{8,7},{9,8},{10,9... | collective-permute-start | bytes 1179656 | tf_op jit(solution)/shard_map/ppermute | solution.py:310
  29.1 2.2 %collective-permute-start = (bf16[240,512]{1,0:T(8,128)(2,1)}, bf16[240,512]{1,0:T(8,128)(2,1)}, u32[]{:S(2)}, u32[]{:S(2)}) collective-permute-start(bf16[240,512]{1,0:T(8,128)(2,1)} %bitcast.20), channel_id=1, source_target_pairs={{0,11},{1,0},{2,1},{3,2},{4,3},{5,4},{6,5},{7,6},{8,7},{9,8},{10,9... | collective-permute-start | bytes 737288 | tf_op jit(solution)/shard_map/ppermute | solution.py:310
  31.2 2.9 %shard_map.113 = f32[8,8,128]{2,1,0:T(8,128)} custom-call(s32[1,3]{1,0:T(1,128)} %bitcast.32, bf16[240,512]{1,0:T(8,128)(2,1)} %bitcast.21, bf16[512,384]{1,0:T(8,128)(2,1)} %get-tuple-element.13.first_ref, bf16[512,384]{1,0:T(8,128)(2,1)} %get-tuple-element.15.second_ref, bf16[240,1024]{1,0:T(8,128)(2,1)} %get-tuple-element.16.dkv_ref), custom_call_target="tpu_custom_call" | custom-call | flops 300000000 | bytes 2000000 | tf_op jit(solution)/shard_map/pallas_call | solution.py:282
  34.1 21.2 %all_to_all.5 = f32[64,1,128]{2,1,0:T(1,128)S(1)} all-to-all(f32[64,1,128]{2,1,0:T(1,128)} %bitcast.25), channel_id=1, replica_groups=mesh['dp'=64,'pipe'=12] {'dp'}, dimensions={0} | all-to-all | bytes 65536 | tf_op jit(solution)/shard_map/all_to_all | solution.py:323
  55.4 0.6 reduce_sum.11
  56.0 3.4 %collective-permute-start.4 = (f32[1,128]{1,0:T(1,128)}, f32[1,128]{1,0:T(1,128)}, u32[]{:S(2)}, u32[]{:S(2)}) collective-permute-start(f32[1,128]{1,0:T(1,128)} %bitcast.10), channel_id=1, source_target_pairs={{0,11},{1,0},{2,1},{3,2},{4,3},{5,4},{6,5},{7,6},{8,7},{9,8},{10,9... | collective-permute-start | bytes 1544 | tf_op jit(solution)/shard_map/ppermute | solution.py:310
  59.3 0.0 collective-permute-done.k_ref
  59.4 0.0 collective-permute-done.2.second_ref
  59.4 0.0 collective-permute-done.1.first_ref
  59.4 4.4 %shard_map.112 = bf16[240,2560]{1,0:T(8,128)(2,1)} custom-call(bf16[240,512]{1,0:T(8,128)(2,1)} %collective-permute-done.k_ref, bf16[512,384]{1,0:T(8,128)(2,1)} %collective-permute-done.1.first_ref, bf16[512,384]{1,0:T(8,128)(2,1)} %collective-permute-done.2.second_ref), custom_call_target="tpu_custom_call" | custom-call | flops 600000000 | bytes 2400000 | tf_op jit(solution)/shard_map/pallas_call | solution.py:270
  63.8 0.0 collective-permute-done.4.sums_ref
  63.8 0.0 collective-permute-done.3.dkv_ref
  63.8 1.8 %shard_map.114 = (bf16[240,512]{1,0:T(8,128)(2,1)}, bf16[240,512]{1,0:T(8,128)(2,1)}, f32[1,48]{1,0:T(1,128)}, f32[1,8]{1,0:T(1,128)}) custom-call(bf16[240,1024]{1,0:T(8,128)(2,1)} %collective-permute-done.3.dkv_ref, f32[1,128]{1,0:T(1,128)} %collective-permute-done.4.sums_ref), custom_call_target="tpu_custom_call" | custom-call | bytes 1000000 | tf_op jit(solution)/shard_map/pallas_call | solution.py:298
Async XLA Ops:
  9.6 54.2 %collective-permute-start.3 = (bf16[240,1024]{1,0:T(8,128)(2,1)}, bf16[240,1024]{1,0:T(8,128)(2,1)}, u32[]{:S(2)}, u32[]{:S(2)}) collective-permute-start(bf16[240,1024]{1,0:T(8,128)(2,1)} %get-tuple-element.16.dkv_ref), channel_id=1, source_target_pairs={{0,11},{1,0},{2,1},{3,2},{4,3},{5,4},{6,5},{7,6},{8,7},{9,8},{10,9... | collective-permute-start | bytes 1474568 | tf_op jit(solution)/shard_map/ppermute | solution.py:310
  24.7 34.7 %collective-permute-start.2 = (bf16[512,384]{1,0:T(8,128)(2,1)}, bf16[512,384]{1,0:T(8,128)(2,1)}, u32[]{:S(2)}, u32[]{:S(2)}) collective-permute-start(bf16[512,384]{1,0:T(8,128)(2,1)} %get-tuple-element.15.second_ref), channel_id=1, source_target_pairs={{0,11},{1,0},{2,1},{3,2},{4,3},{5,4},{6,5},{7,6},{8,7},{9,8},{10,9... | collective-permute-start | bytes 1179656 | tf_op jit(solution)/shard_map/ppermute | solution.py:310
  26.9 32.5 %collective-permute-start.1 = (bf16[512,384]{1,0:T(8,128)(2,1)}, bf16[512,384]{1,0:T(8,128)(2,1)}, u32[]{:S(2)}, u32[]{:S(2)}) collective-permute-start(bf16[512,384]{1,0:T(8,128)(2,1)} %get-tuple-element.13.first_ref), channel_id=1, source_target_pairs={{0,11},{1,0},{2,1},{3,2},{4,3},{5,4},{6,5},{7,6},{8,7},{9,8},{10,9... | collective-permute-start | bytes 1179656 | tf_op jit(solution)/shard_map/ppermute | solution.py:310
  29.1 30.3 %collective-permute-start = (bf16[240,512]{1,0:T(8,128)(2,1)}, bf16[240,512]{1,0:T(8,128)(2,1)}, u32[]{:S(2)}, u32[]{:S(2)}) collective-permute-start(bf16[240,512]{1,0:T(8,128)(2,1)} %bitcast.20), channel_id=1, source_target_pairs={{0,11},{1,0},{2,1},{3,2},{4,3},{5,4},{6,5},{7,6},{8,7},{9,8},{10,9... | collective-permute-start | bytes 737288 | tf_op jit(solution)/shard_map/ppermute | solution.py:310
  56.0 7.8 %collective-permute-start.4 = (f32[1,128]{1,0:T(1,128)}, f32[1,128]{1,0:T(1,128)}, u32[]{:S(2)}, u32[]{:S(2)}) collective-permute-start(f32[1,128]{1,0:T(1,128)} %bitcast.10), channel_id=1, source_target_pairs={{0,11},{1,0},{2,1},{3,2},{4,3},{5,4},{6,5},{7,6},{8,7},{9,8},{10,9... | collective-permute-start | bytes 1544 | tf_op jit(solution)/shard_map/ppermute | solution.py:310

commit v2 on v1

v2 whole, which is shorter than its diff:
```python
import functools
import math

import jax
import jax.numpy as jnp
from jax import lax
from jax.experimental import pallas as pl
from jax.experimental.pallas import tpu as pltpu
from jax.sharding import PartitionSpec as P


HEADS = 20
KV_HEADS = 4
HEAD_DIM = 128
PER_GROUP = HEADS // KV_HEADS
CANDIDATES = 3
LONGEST = 80
HOME_ROWS = 240
PAIR = 2
WIDTH = PER_GROUP * LONGEST
MAIN = WIDTH // 128 * 128
REST = WIDTH - MAIN
CHUNK = HOME_ROWS + REST
TILES = MAIN // 128
FACTOR = 1.0 / math.sqrt(HEAD_DIM)
BF16 = jnp.bfloat16
F32 = jnp.float32


def dot(left, right, left_dim=1, right_dim=0):
    return lax.dot_general(
        left, right, (((left_dim,), (right_dim,)), ((), ())), preferred_element_type=F32
    )


def iota(shape, axis):
    return lax.broadcasted_iota(jnp.int32, shape, axis)


def spans(lengths):
    starts = [jnp.zeros_like(lengths[0])]
    for c in range(CANDIDATES - 1):
        starts.append(starts[-1] + lengths[c])
    return starts, lengths


def stored_spans(lengths_ref):
    return spans([lengths_ref[0, c] for c in range(CANDIDATES)])


SCORE_ROWS = PAIR * TILES * CHUNK
GRAD_ROWS = 2 * PAIR * HOME_ROWS
FIRST = (SCORE_ROWS, 128)
SECOND = (GRAD_ROWS + SCORE_ROWS + GRAD_ROWS, 128)


def tile(g, m):
    return (g * TILES + m) * CHUNK


def grads_at(at):
    return slice(at * HOME_ROWS, (at + 1) * HOME_ROWS)


def sent_spans(ref):
    start = tile(0, TILES - 1) + HOME_ROWS
    corner = ref[start : start + REST, :].astype(F32).astype(jnp.int32)
    return spans([corner[c : c + 1, :1] for c in range(CANDIDATES)])


def total(rows):
    return jnp.sum(rows.astype(F32), axis=0, keepdims=True)


def one_hot(hit):
    return jnp.where(hit, 1.0, 0.0).astype(BF16)


def to_slots(found):
    starts, lengths = found
    shape = (LONGEST, HOME_ROWS)
    row, home = iota(shape, 0), iota(shape, 1)
    return jnp.concatenate(
        [one_hot((home == row + starts[c]) & (row < lengths[c])) for c in range(CANDIDATES)], axis=0
    )


def to_home(found):
    starts, lengths = found
    shape = (HOME_ROWS, HOME_ROWS)
    home, slot = iota(shape, 0), iota(shape, 1)
    hit = jnp.zeros(shape, jnp.bool_)
    for c in range(CANDIDATES):
        j = slot - c * LONGEST
        hit = hit | ((home == j + starts[c]) & (j >= 0) & (j < lengths[c]))
    return one_hot(hit)


def rows_of(tensor, c):
    return tensor[c * LONGEST : (c + 1) * LONGEST]


def stacked(tensor, g, c):
    part = rows_of(tensor, c)
    base = g * PER_GROUP
    return jnp.concatenate(
        [part[:, (base + h) * HEAD_DIM : (base + h + 1) * HEAD_DIM] for h in range(PER_GROUP)], axis=0
    )


def scores_kernel(
    pair, lengths_ref, q_ref, k_ref, v_ref, o_ref, norm_ref, delta_ref, *refs
):
    if pair == 0:
        earlier_ref, (out_ref, grads_ref, sums_ref) = None, refs
    else:
        earlier_ref, _, both_ref, sums_ref = refs
        out_ref, grads_ref = both_ref.at[:SCORE_ROWS], both_ref.at[SCORE_ROWS:]
    found = stored_spans(lengths_ref)
    slots, home = to_slots(found), to_home(found)
    q = dot(slots, q_ref[...]).astype(BF16)
    k = dot(slots, k_ref[...]).astype(BF16)
    v = dot(slots, v_ref[...]).astype(BF16)
    o = dot(slots, o_ref[...]).astype(BF16)
    starts, lengths = found
    shape = (HOME_ROWS, WIDTH)
    at, lane = iota(shape, 0), iota(shape, 1)
    head_of = iota((PER_GROUP, WIDTH), 1)
    own = (head_of >= iota((PER_GROUP, WIDTH), 0) * LONGEST) & (
        head_of < (iota((PER_GROUP, WIDTH), 0) + 1) * LONGEST
    )
    within = lane
    for h in range(1, PER_GROUP):
        within = jnp.where(lane >= h * LONGEST, lane - h * LONGEST, within)
    head_at, head_lane = iota((WIDTH, 128), 0), iota((WIDTH, 128), 1) * LONGEST
    heads = one_hot((head_at >= head_lane) & (head_at < head_lane + LONGEST))
    per_head = [[] for _ in range(PAIR)]
    rest = [[] for _ in range(PAIR)]
    dk = [[] for _ in range(PAIR)]
    dv = [[] for _ in range(PAIR)]
    for c in range(CANDIDATES):
        spread = one_hot((at == within + starts[c]) & (within < lengths[c]))
        norms = dot(norm_ref[...], spread)
        deltas = dot(delta_ref[...], spread)
        for g in range(PAIR):
            base = (pair * PAIR + g) * PER_GROUP
            norm = jnp.sum(jnp.where(own, norms[base : base + PER_GROUP], 0.0), axis=0, keepdims=True)
            delta = jnp.sum(jnp.where(own, deltas[base : base + PER_GROUP], 0.0), axis=0, keepdims=True)
            q_rows, o_rows = stacked(q, g, c), stacked(o, g, c)
            k_part = rows_of(k, c)[:, g * HEAD_DIM : (g + 1) * HEAD_DIM]
            v_part = rows_of(v, c)[:, g * HEAD_DIM : (g + 1) * HEAD_DIM]
            probs = jnp.exp(dot(k_part, q_rows, 1, 1) * FACTOR - norm)
            dscores = probs * (dot(v_part, o_rows, 1, 1) - delta)
            probs_low, dscores_low = probs.astype(BF16), dscores.astype(BF16)
            dk[g].append(dot(dscores_low, q_rows) * FACTOR)
            dv[g].append(dot(probs_low, o_rows))
            per_head[g].append(dot(dscores_low, heads))
            for m in range(TILES):
                start = tile(g, m) + c * LONGEST
                out_ref[start : start + LONGEST, :] = dscores_low[:, m * 128 : (m + 1) * 128]
            rest[g].append(dscores[:, MAIN:])
    sums = [[], [], []]
    for g in range(PAIR):
        for at, grads in ((g, dk[g]), (PAIR + g, dv[g])):
            rows = dot(home, jnp.concatenate(grads, axis=0).astype(BF16)).astype(BF16)
            grads_ref[grads_at(at), :] = rows
            sums[1 + at // PAIR].append(total(rows))
        scores = jnp.concatenate(per_head[g], axis=0)
        coarse = scores.astype(BF16)
        scores = jnp.concatenate([coarse, (scores - coarse.astype(F32)).astype(BF16)], axis=0)
        keys = k[:, g * HEAD_DIM : (g + 1) * HEAD_DIM]
        queries = dot(scores, jnp.concatenate([keys, keys], axis=0), 0, 0) * FACTOR
        sums[0] += [queries[h : h + 1] for h in range(PER_GROUP)]
        turned = jnp.concatenate(rest[g], axis=0).T.astype(BF16)
        corner = jnp.zeros((REST, 128), F32)
        for c in range(CANDIDATES):
            corner = jnp.where(iota(corner.shape, 0) == c, lengths[c].astype(F32), corner)
        pad = jnp.zeros((REST, (TILES - 1) * 128 - HOME_ROWS), BF16)
        turned = jnp.concatenate([turned, pad, corner.astype(BF16)], axis=1)
        for m in range(TILES):
            start = tile(g, m) + HOME_ROWS
            out_ref[start : start + REST, :] = turned[:, m * 128 : (m + 1) * 128]
    sums = [jnp.concatenate(row, axis=1) for row in sums]
    if earlier_ref is None:
        sums_ref[...] = jnp.concatenate(sums, axis=1)
    else:
        before = earlier_ref[...]
        parts = before[:, :QW], before[:, QW : QW + KW], before[:, QW + KW :]
        both = [row for pair_of in zip(parts, sums) for row in pair_of]
        fill_pieces(sums_ref, jnp.concatenate(both[:4], axis=1), jnp.concatenate(both[4:], axis=1))


def query_grads(ref, g, k_group):
    def lines(start, rows):
        at = [tile(g, m) + start for m in range(TILES)]
        return jnp.concatenate([ref[a : a + rows, :] for a in at], axis=1)

    turned = lines(HOME_ROWS, REST)[:, :HOME_ROWS]
    lane = iota((REST, HOME_ROWS), 1)
    found = []
    for c in range(CANDIDATES):
        main = dot(lines(c * LONGEST, LONGEST), rows_of(k_group, c), 0, 0)
        mine = (lane >= c * LONGEST) & (lane < (c + 1) * LONGEST)
        last = dot(jnp.where(mine, turned.astype(F32), 0.0).astype(BF16), k_group)
        rows = (jnp.concatenate([main, last], axis=0) * FACTOR).astype(BF16)
        found.append(
            jnp.concatenate([rows[h * LONGEST : (h + 1) * LONGEST] for h in range(PER_GROUP)], axis=1)
        )
    return jnp.concatenate(found, axis=0)


def queries_kernel(k_ref, parcel_ref, q_out):
    found = sent_spans(parcel_ref)
    k = dot(to_slots(found), k_ref[...]).astype(BF16)
    home = to_home(found)
    width = PER_GROUP * HEAD_DIM
    for g in range(PAIR):
        rows = query_grads(parcel_ref, g, k[:, g * HEAD_DIM : (g + 1) * HEAD_DIM])
        q_out[:, g * width : (g + 1) * width] = dot(home, rows).astype(BF16)


def last_kernel(k_ref, parcel_ref, spread_ref, _, q_out, k_out, v_out, bias_ref, value_bias_ref):
    queries_kernel(k_ref, parcel_ref.at[GRAD_ROWS : GRAD_ROWS + SCORE_ROWS], q_out)
    for pair in range(KV_HEADS // PAIR):
        grads = parcel_ref.at[pair * (GRAD_ROWS + SCORE_ROWS) : pair * (GRAD_ROWS + SCORE_ROWS) + GRAD_ROWS]
        for g in range(PAIR):
            at = (pair * PAIR + g) * HEAD_DIM
            k_out[:, at : at + HEAD_DIM] = grads[grads_at(g), :]
            v_out[:, at : at + HEAD_DIM] = grads[grads_at(PAIR + g), :]
    sums = total(spread_ref[...])
    step = bias_ref.shape[1]
    bias_ref[...] = sums[:, :step]
    value_bias_ref[...] = sums[:, step : step + value_bias_ref.shape[1]]


def fill_pieces(out_ref, sums, value_sums):
    ranks = out_ref.shape[0] * out_ref.shape[1]
    step, value_step = sums.shape[1] // ranks, value_sums.shape[1] // ranks

    def folded(row, width):
        return jnp.concatenate([row[:, i * width : (i + 1) * width] for i in reversed(range(8))], axis=0)

    sums = folded(sums, 8 * step)
    pad = jnp.zeros((8, 128 - 8 * value_step), F32)
    value_sums = jnp.concatenate([folded(value_sums, 8 * value_step), pad], axis=1)
    lane = iota((8, 128), 1)
    for p in range(8):
        left = pltpu.roll(sums, (sums.shape[1] - step * p) % sums.shape[1], 1)[:, :128]
        right = pltpu.roll(value_sums, (step - value_step * p) % 128, 1)
        out_ref[:, 7 - p, :] = jnp.where(
            lane < step, left, jnp.where(lane < step + value_step, right, 0.0)
        )


VMEM_LIMIT = 67_043_328
SMEM = pl.BlockSpec(memory_space=pltpu.SMEM)


def whole(shape):
    return pl.BlockSpec(shape, lambda i: (0,) * len(shape))


def columns(width, at):
    return pl.BlockSpec((HOME_ROWS, width), lambda i: (0, at))


QW = PAIR * PER_GROUP * HEAD_DIM
KW = PAIR * HEAD_DIM


def kernel(body, flops, moved, exps=0, steps=1, **rest):
    return pl.pallas_call(
        body,
        grid=(steps,),
        cost_estimate=pl.CostEstimate(flops=flops, bytes_accessed=moved, transcendentals=exps),
        compiler_params=pltpu.CompilerParams(vmem_limit_bytes=VMEM_LIMIT),
        **rest,
    )


ANY = pl.BlockSpec(memory_space=pl.ANY)


def score_grads(pair, ranks, lengths, q, k, v, o, norm, delta, earlier):
    shape = jax.ShapeDtypeStruct
    if pair == 0:
        sums = (1, QW + 2 * KW)
        outs = (shape(FIRST, BF16), shape(SECOND, BF16), shape(sums, F32))
        out_specs = (whole(FIRST), pl.BlockSpec((GRAD_ROWS, 128), lambda i: (0, 0)), whole(sums))
        extra, extra_specs, aliases = (), [], {}
    else:
        sums = (8, ranks // 8, 128)
        outs = (shape(SECOND, BF16), shape(sums, F32))
        rows = pl.BlockSpec(
            (pl.Element(SCORE_ROWS + GRAD_ROWS), pl.Element(128)), lambda i: (GRAD_ROWS, 0)
        )
        out_specs = (rows, whole(sums))
        extra, extra_specs, aliases = earlier, [whole(earlier[0].shape), ANY], {8: 0}
    return kernel(
        functools.partial(scores_kernel, pair),
        800_000_000,
        2_400_000,
        400_000,
        out_shape=outs,
        in_specs=[
            SMEM,
            columns(QW, pair),
            columns(KW, pair),
            columns(KW, pair),
            columns(QW, pair),
            whole((HEADS, HOME_ROWS)),
            whole((HEADS, HOME_ROWS)),
        ]
        + extra_specs,
        out_specs=out_specs,
        input_output_aliases=aliases,
    )(lengths, q, k, v, o, norm, delta, *extra)


def first_queries(k, parcel):
    return kernel(
        queries_kernel,
        300_000_000,
        1_600_000,
        out_shape=jax.ShapeDtypeStruct((HOME_ROWS, HEADS * HEAD_DIM), BF16),
        in_specs=[columns(KW, 0), whole(FIRST)],
        out_specs=columns(QW, 0),
    )(k, parcel)


def last_outputs(k, parcel, spread, up_q):
    shape = jax.ShapeDtypeStruct
    wide = KV_HEADS * HEAD_DIM
    ranks = spread.shape[0]
    small = ((HEADS + KV_HEADS) * HEAD_DIM // ranks, wide // ranks)
    return kernel(
        last_kernel,
        300_000_000,
        2_000_000,
        out_shape=(
            (shape((HOME_ROWS, HEADS * HEAD_DIM), BF16),)
            + (shape((HOME_ROWS, wide), BF16),) * 2
            + tuple(shape((1, n), F32) for n in small)
        ),
        in_specs=[columns(KW, 1), whole(SECOND), whole(spread.shape), ANY],
        out_specs=(columns(QW, 1),) + (whole((HOME_ROWS, wide)),) * 2 + tuple(whole((1, n)) for n in small),
        input_output_aliases={3: 0},
    )(k, parcel, spread, up_q)


def up(value):
    count = lax.axis_size("pipe")
    return lax.ppermute(value, "pipe", [(s, (s - 1) % count) for s in range(count)])


def relay(q, k, v, o, norm, delta, lengths):
    ranks = lax.axis_size("dp")
    k_up = up(k)
    first, second, sums = score_grads(0, ranks, lengths, q, k, v, o, norm, delta, None)
    first = up(first)
    second, sums = score_grads(1, ranks, lengths, q, k, v, o, norm, delta, (sums, second))
    sums = up(sums)
    second = up(second)
    backward = [list(reversed(range(ranks)))]
    spread = lax.all_to_all(
        sums.reshape(ranks, 1, 128), "dp", 0, 0, axis_index_groups=backward, tiled=True
    )
    up_q = first_queries(k_up, first)
    return last_outputs(k_up, second, spread.reshape(ranks, 128), up_q)


def shards(queries, key_rows, value_rows, out_grad, log_norm, row_delta, cand_lengths):
    up_q, up_k, up_v, bias, value_bias = relay(
        queries[0], key_rows[0], value_rows[0], out_grad[0], log_norm[0], row_delta[0], cand_lengths[0]
    )
    return up_q[None], up_k[None], up_v[None], bias, value_bias


def solution(mesh):
    in_specs = (
        P("pipe", "dp", None),
        P("pipe", "dp", None),
        P("pipe", "dp", None),
        P("pipe", "dp", None),
        P("pipe", None, "dp"),
        P("pipe", None, "dp"),
        P("pipe", "dp", None),
    )
    out_specs = (
        P("pipe", "dp", None),
        P("pipe", "dp", None),
        P("pipe", "dp", None),
        P("pipe", "dp"),
        P("pipe", "dp"),
    )
    return jax.shard_map(shards, mesh=mesh, in_specs=in_specs, out_specs=out_specs, check_vma=False)
```

time: 66.1 us -> 79.8 us (1.21)
  waiting for transfers between devices: 0.01 us -> 28.7 us
  blocking collectives: 21.2 us -> 0 us
  starting transfers between devices: 25 us -> 34.3 us
  Pallas kernels: 18.1 us -> 15.7 us
    ppermute x5 -> x4, waiting for transfers between devices: 0.01 us -> 26.4 us  [up(): lax.ppermute(value, 'pipe', [(s, (s - 1) % count) for s in range(count)])]
    all_to_all x1 -> x0, blocking collectives: 21.2 us -> none  [relay(): lax.all_to_all(pieces.reshape(ranks, 1, 128), 'dp', 0, 0, tiled=True)]
    all_to_all x0 -> x1, starting transfers between devices: none -> 12.6 us  [relay(): lax.all_to_all(sums.reshape(ranks, 1, 128), 'dp', 0, 0, axis_index_groups...]
    ppermute x5 -> x4, starting transfers between devices: 25 us -> 21.7 us  [up(): lax.ppermute(value, 'pipe', [(s, (s - 1) % count) for s in range(count)])]
    pallas_call x3 -> x2, Pallas kernels: 9.13 us -> 6.05 us  [the longest x1 3.15 us: last_outputs(): kernel(last_kernel, 300000000, 2000000, out_shape=(shape((HOME_ROWS, HEAD...]
    all_to_all x0 -> x1, waiting for transfers between devices: none -> 2.28 us  [relay(): lax.all_to_all(sums.reshape(ranks, 1, 128), 'dp', 0, 0, axis_index_groups...]
  transfers between devices with their start and end apart: 5 -> 5, of which waited for: 0 -> 2; matrix products, arithmetic and copies ran while one was open for 1% -> 0% of each run, Pallas kernels for 11% -> 4%
where the time goes in v2:
time: 79.8 us; the launch traced here: 79.4 us
  starting transfers between devices  34.3 us (43%)
  waiting for transfers between devices  28.7 us (36%)
  Pallas kernels  15.7 us (20%)
    ppermute x4, waiting for transfers between devices, up(): lax.ppermute(value, 'pipe', [(s, (s - 1) % count) for s in range(count)])  26.4 us
    ppermute x4, starting transfers between devices, up(): lax.ppermute(value, 'pipe', [(s, (s - 1) % count) for s in range(count)])  21.7 us
    all_to_all x1, starting transfers between devices, relay(): lax.all_to_all(sums.reshape(ranks, 1, 128), 'dp', 0, 0, axis_index_groups...  12.6 us
    pallas_call x2, Pallas kernels, score_grads(): kernel(functools.partial(scores_kernel, pair), 800000000, 2400000, 400000...  9.67 us
    pallas_call x1, Pallas kernels, last_outputs(): kernel(last_kernel, 300000000, 2000000, out_shape=(shape((HOME_ROWS, HEAD...  3.15 us
    pallas_call x1, Pallas kernels, first_queries(): kernel(queries_kernel, 300000000, 1600000, out_shape=jax.ShapeDtypeStruct...  2.91 us
    all_to_all x1, waiting for transfers between devices, relay(): lax.all_to_all(sums.reshape(ranks, 1, 128), 'dp', 0, 0, axis_index_groups...  2.28 us
  transfers between devices with their start and end apart: 5, of which 2 were waited for; matrix products, arithmetic and copies ran while one was open for 0% of the time, Pallas kernels for 4%

profile of v2, /device:TPU:1, one launch (start us, length us, event | category | flops | bytes accessed | tf_op | source)
XLA Modules:
  0.0 79.4 jit_solution(18175981161991960526)
XLA Ops:
  0.6 4.7 %shard_map.110 = (bf16[1536,128]{1,0:T(8,128)(2,1)}, bf16[3456,128]{1,0:T(8,128)(2,1)}, f32[1,1792]{1,0:T(1,128)}) custom-call(s32[1,3]{1,0:T(1,128)} %bitcast.28, bf16[240,2560]{1,0:T(8,128)(2,1)} %bitcast.14, bf16[240,512]{1,0:T(8,128)(2,1)} %bitcast.21, bf16[240,512]{1,0:T(8,128)(2,1)} %bitcast.19, bf16[240,2560]{1,0:T(8,128)(2,1)} %bitcast.16, ...), custom_call_target="tpu_custom_call" | custom-call | flops 800000000 | bytes 2400000 | tf_op jit(solution)/shard_map/pallas_call | solution.py:299
  5.3 5.0 %shard_map.111 = (bf16[3456,128]{1,0:T(8,128)(2,1)}, f32[8,8,128]{2,1,0:T(8,128)}) custom-call(s32[1,3]{1,0:T(1,128)} %bitcast.29, bf16[240,2560]{1,0:T(8,128)(2,1)} %bitcast.15, bf16[240,512]{1,0:T(8,128)(2,1)} %bitcast.22, bf16[240,512]{1,0:T(8,128)(2,1)} %bitcast.20, bf16[240,2560]{1,0:T(8,128)(2,1)} %bitcast.17, ...), custom_call_target="tpu_custom_call", output_to_operand_aliasing={{0}: (8, {})} | custom-call | flops 800000000 | bytes 2400000 | tf_op jit(solution)/shard_map/pallas_call | solution.py:299
  10.3 15.1 %collective-permute-start.1 = (bf16[3456,128]{1,0:T(8,128)(2,1)}, bf16[3456,128]{1,0:T(8,128)(2,1)}, u32[]{:S(2)}, u32[]{:S(2)}) collective-permute-start(bf16[3456,128]{1,0:T(8,128)(2,1)} %get-tuple-element.17), channel_id=1, source_target_pairs={{0,11},{1,0},{2,1},{3,2},{4,3},{5,4},{6,5},{7,6},{8,7},{9,8},{10,9... | collective-permute-start | bytes 2654216 | tf_op jit(solution)/shard_map/ppermute | solution.py:353
  25.4 2.2 %collective-permute-start.3 = (bf16[1536,128]{1,0:T(8,128)(2,1)}, bf16[1536,128]{1,0:T(8,128)(2,1)}, u32[]{:S(2)}, u32[]{:S(2)}) collective-permute-start(bf16[1536,128]{1,0:T(8,128)(2,1)} %get-tuple-element.19), channel_id=1, source_target_pairs={{0,11},{1,0},{2,1},{3,2},{4,3},{5,4},{6,5},{7,6},{8,7},{9,8},{10,9... | collective-permute-start | bytes 1179656 | tf_op jit(solution)/shard_map/ppermute | solution.py:353
  27.6 2.2 %collective-permute-start = (bf16[240,512]{1,0:T(8,128)(2,1)}, bf16[240,512]{1,0:T(8,128)(2,1)}, u32[]{:S(2)}, u32[]{:S(2)}) collective-permute-start(bf16[240,512]{1,0:T(8,128)(2,1)} %bitcast.23), channel_id=1, source_target_pairs={{0,11},{1,0},{2,1},{3,2},{4,3},{5,4},{6,5},{7,6},{8,7},{9,8},{10,9... | collective-permute-start | bytes 737288 | tf_op jit(solution)/shard_map/ppermute | solution.py:353
  29.8 2.2 %collective-permute-start.2 = (f32[8,8,128]{2,1,0:T(8,128)}, f32[8,8,128]{2,1,0:T(8,128)}, u32[]{:S(2)}, u32[]{:S(2)}) collective-permute-start(f32[8,8,128]{2,1,0:T(8,128)} %get-tuple-element.18), channel_id=1, source_target_pairs={{0,11},{1,0},{2,1},{3,2},{4,3},{5,4},{6,5},{7,6},{8,7},{9,8},{10,9... | collective-permute-start | bytes 98312 | tf_op jit(solution)/shard_map/ppermute | solution.py:353
  32.0 26.4 %collective-permute-done.2 = f32[8,8,128]{2,1,0:T(8,128)} collective-permute-done((f32[8,8,128]{2,1,0:T(8,128)}, f32[8,8,128]{2,1,0:T(8,128)}, u32[]{:S(2)}, u32[]{:S(2)}) %collective-permute-start.2) | collective-permute-done | bytes 32800 | tf_op jit(solution)/shard_map/ppermute | solution.py:353
  58.4 12.6 %all-to-all-start = ((f32[64,1,128]{2,1,0:T(1,128)}), f32[64,1,128]{2,1,0:T(1,128)}, u32[]{:S(2)}, u32[]{:S(2)}) async-start(f32[64,1,128]{2,1,0:T(1,128)} %bitcast.8), calls=%async_computation | async-start | bytes 65536 | tf_op jit(solution)/shard_map/all_to_all | solution.py:365
  71.1 0.0 collective-permute-done.k_ref
  71.1 0.0 collective-permute-done.3.parcel_ref
  71.1 2.9 %shard_map.112._ = bf16[240,2560]{1,0:T(8,128)(2,1)} custom-call(bf16[240,512]{1,0:T(8,128)(2,1)} %collective-permute-done.k_ref, bf16[1536,128]{1,0:T(8,128)(2,1)} %collective-permute-done.3.parcel_ref), custom_call_target="tpu_custom_call" | custom-call | flops 300000000 | bytes 1600000 | tf_op jit(solution)/shard_map/pallas_call | solution.py:321
  74.0 2.3 %all-to-all-done = f32[64,1,128]{2,1,0:T(1,128)} async-done(((f32[64,1,128]{2,1,0:T(1,128)}), f32[64,1,128]{2,1,0:T(1,128)}, u32[]{:S(2)}, u32[]{:S(2)}) %all-to-all-start) | async-done | bytes 32800 | tf_op jit(solution)/shard_map/all_to_all | solution.py:365
  76.3 0.0 collective-permute-done.1.parcel_ref
  76.3 3.1 %shard_map.113 = (bf16[240,2560]{1,0:T(8,128)(2,1)}, bf16[240,512]{1,0:T(8,128)(2,1)}, bf16[240,512]{1,0:T(8,128)(2,1)}, f32[1,48]{1,0:T(1,128)}, f32[1,8]{1,0:T(1,128)}) custom-call(bf16[240,512]{1,0:T(8,128)(2,1)} %collective-permute-done.k_ref, bf16[3456,128]{1,0:T(8,128)(2,1)} %collective-permute-done.1.parcel_ref, ...), custom_call_target="tpu_custom_call", output_to_operand_aliasing={{0}: (3, {})} | custom-call | flops 300000000 | bytes 2000000 | tf_op jit(solution)/shard_map/pallas_call | solution.py:336
Async XLA Ops:
  10.3 66.0 %collective-permute-start.1 = (bf16[3456,128]{1,0:T(8,128)(2,1)}, bf16[3456,128]{1,0:T(8,128)(2,1)}, u32[]{:S(2)}, u32[]{:S(2)}) collective-permute-start(bf16[3456,128]{1,0:T(8,128)(2,1)} %get-tuple-element.17), channel_id=1, source_target_pairs={{0,11},{1,0},{2,1},{3,2},{4,3},{5,4},{6,5},{7,6},{8,7},{9,8},{10,9... | collective-permute-start | bytes 2654216 | tf_op jit(solution)/shard_map/ppermute | solution.py:353
  25.4 45.7 %collective-permute-start.3 = (bf16[1536,128]{1,0:T(8,128)(2,1)}, bf16[1536,128]{1,0:T(8,128)(2,1)}, u32[]{:S(2)}, u32[]{:S(2)}) collective-permute-start(bf16[1536,128]{1,0:T(8,128)(2,1)} %get-tuple-element.19), channel_id=1, source_target_pairs={{0,11},{1,0},{2,1},{3,2},{4,3},{5,4},{6,5},{7,6},{8,7},{9,8},{10,9... | collective-permute-start | bytes 1179656 | tf_op jit(solution)/shard_map/ppermute | solution.py:353
  27.6 43.4 %collective-permute-start = (bf16[240,512]{1,0:T(8,128)(2,1)}, bf16[240,512]{1,0:T(8,128)(2,1)}, u32[]{:S(2)}, u32[]{:S(2)}) collective-permute-start(bf16[240,512]{1,0:T(8,128)(2,1)} %bitcast.23), channel_id=1, source_target_pairs={{0,11},{1,0},{2,1},{3,2},{4,3},{5,4},{6,5},{7,6},{8,7},{9,8},{10,9... | collective-permute-start | bytes 737288 | tf_op jit(solution)/shard_map/ppermute | solution.py:353
  29.8 28.6 %collective-permute-start.2 = (f32[8,8,128]{2,1,0:T(8,128)}, f32[8,8,128]{2,1,0:T(8,128)}, u32[]{:S(2)}, u32[]{:S(2)}) collective-permute-start(f32[8,8,128]{2,1,0:T(8,128)} %get-tuple-element.18), channel_id=1, source_target_pairs={{0,11},{1,0},{2,1},{3,2},{4,3},{5,4},{6,5},{7,6},{8,7},{9,8},{10,9... | collective-permute-start | bytes 98312 | tf_op jit(solution)/shard_map/ppermute | solution.py:353
  58.4 17.8 %all-to-all-start = ((f32[64,1,128]{2,1,0:T(1,128)}), f32[64,1,128]{2,1,0:T(1,128)}, u32[]{:S(2)}, u32[]{:S(2)}) async-start(f32[64,1,128]{2,1,0:T(1,128)} %bitcast.8), calls=%async_computation | async-start | bytes 65536 | tf_op jit(solution)/shard_map/all_to_all | solution.py:365

commit v3 on v2

--- a/solution.py
+++ b/solution.py
@@ -252,7 +252,7 @@
         )
 
 
-VMEM_LIMIT = 67_043_328
+SOME_VMEM = 24 * 2**20
 SMEM = pl.BlockSpec(memory_space=pltpu.SMEM)
 
 
@@ -268,12 +268,12 @@
 KW = PAIR * HEAD_DIM
 
 
-def kernel(body, flops, moved, exps=0, steps=1, **rest):
+def kernel(body, limit, flops, moved, exps=0, **rest):
     return pl.pallas_call(
         body,
-        grid=(steps,),
+        grid=(1,),
         cost_estimate=pl.CostEstimate(flops=flops, bytes_accessed=moved, transcendentals=exps),
-        compiler_params=pltpu.CompilerParams(vmem_limit_bytes=VMEM_LIMIT),
+        compiler_params=pltpu.CompilerParams(vmem_limit_bytes=limit),
         **rest,
     )
 
@@ -298,6 +298,7 @@
         extra, extra_specs, aliases = earlier, [whole(earlier[0].shape), ANY], {8: 0}
     return kernel(
         functools.partial(scores_kernel, pair),
+        (60 * 2**20, 24 * 2**20)[pair],
         800_000_000,
         2_400_000,
         400_000,
@@ -320,6 +321,7 @@
 def first_queries(k, parcel):
     return kernel(
         queries_kernel,
+        SOME_VMEM,
         300_000_000,
         1_600_000,
         out_shape=jax.ShapeDtypeStruct((HOME_ROWS, HEADS * HEAD_DIM), BF16),
@@ -335,6 +337,7 @@
     small = ((HEADS + KV_HEADS) * HEAD_DIM // ranks, wide // ranks)
     return kernel(
         last_kernel,
+        SOME_VMEM,
         300_000_000,
         2_000_000,
         out_shape=(

time: 79.8 us -> 78.4 us (0.982)
  Pallas kernels: 15.7 us -> 12.7 us
  waiting for transfers between devices: 28.7 us -> 29.8 us
    pallas_call x4, Pallas kernels: 15.7 us -> 12.7 us  [the longest x2 8.88 us: score_grads(): kernel(functools.partial(scores_kernel, pair), (60 * 2 ** 20, 24 * 2 ** 2...]
    all_to_all x1, waiting for transfers between devices: 2.28 us -> 3.43 us  [relay(): lax.all_to_all(sums.reshape(ranks, 1, 128), 'dp', 0, 0, axis_index_groups...]
  transfers between devices with their start and end apart: 5 -> 5, of which waited for: 2 -> 2; matrix products, arithmetic and copies ran while one was open for 0% -> 0% of each run, Pallas kernels for 4% -> 2%
where the time goes in v3:
time: 78.4 us; the launch traced here: 78.1 us
  starting transfers between devices  34.1 us (43%)
  waiting for transfers between devices  29.8 us (38%)
  Pallas kernels  12.7 us (16%)
  between operations  0.81 us (1%)
    ppermute x4, waiting for transfers between devices, up(): lax.ppermute(value, 'pipe', [(s, (s - 1) % count) for s in range(count)])  26.3 us
    ppermute x4, starting transfers between devices, up(): lax.ppermute(value, 'pipe', [(s, (s - 1) % count) for s in range(count)])  21.7 us
    all_to_all x1, starting transfers between devices, relay(): lax.all_to_all(sums.reshape(ranks, 1, 128), 'dp', 0, 0, axis_index_groups...  12.4 us
    pallas_call x2, Pallas kernels, score_grads(): kernel(functools.partial(scores_kernel, pair), (60 * 2 ** 20, 24 * 2 ** 2...  8.88 us
    all_to_all x1, waiting for transfers between devices, relay(): lax.all_to_all(sums.reshape(ranks, 1, 128), 'dp', 0, 0, axis_index_groups...  3.43 us
    pallas_call x1, Pallas kernels, last_outputs(): kernel(last_kernel, SOME_VMEM, 300000000, 2000000, out_shape=(shape((HOME...  1.98 us
    pallas_call x1, Pallas kernels, first_queries(): kernel(queries_kernel, SOME_VMEM, 300000000, 1600000, out_shape=jax.Shape...  1.84 us
  transfers between devices with their start and end apart: 5, of which 2 were waited for; matrix products, arithmetic and copies ran while one was open for 0% of the time, Pallas kernels for 2%

profile of v3, /device:TPU:1, one launch (start us, length us, event | category | flops | bytes accessed | tf_op | source)
XLA Modules:
  0.0 78.1 jit_solution(14542755628817384588)
XLA Ops:
  0.6 0.0 copy-start
  0.6 0.0 copy-start.1
  0.7 0.0 copy-start.2
  0.7 0.0 copy-start.3
  0.7 0.0 copy-start.4
  0.7 0.0 copy-start.5
  0.7 0.0 copy-start.7
  0.7 4.8 %shard_map.110 = (bf16[1536,128]{1,0:T(8,128)(2,1)}, bf16[3456,128]{1,0:T(8,128)(2,1)}, f32[1,1792]{1,0:T(1,128)}) custom-call(s32[1,3]{1,0:T(1,128)} %bitcast.28, bf16[240,2560]{1,0:T(8,128)(2,1)} %bitcast.14, bf16[240,512]{1,0:T(8,128)(2,1)} %bitcast.20, bf16[240,512]{1,0:T(8,128)(2,1)} %bitcast.18, bf16[240,2560]{1,0:T(8,128)(2,1)} %bitcast.16, ...), custom_call_target="tpu_custom_call" | custom-call | flops 800000000 | bytes 2400000 | tf_op jit(solution)/shard_map/pallas_call | solution.py:299
  5.5 0.0 copy-done
  5.5 0.0 copy-done.1
  5.6 0.0 copy-done.2
  5.6 0.0 copy-done.3
  5.6 0.0 copy-done.4
  5.6 0.0 copy-done.5
  5.6 0.0 copy-done.7
  5.6 0.0 copy-start.6
  5.6 0.7 copy-done.6
  6.3 0.0 copy-start.8
  6.3 4.0 %shard_map.111 = (bf16[3456,128]{1,0:T(8,128)(2,1)}, f32[8,8,128]{2,1,0:T(8,128)S(1)}) custom-call(s32[1,3]{1,0:T(1,128)S(1)} %bitcast.29, bf16[240,2560]{1,0:T(8,128)(2,1)S(1)} %bitcast.15, bf16[240,512]{1,0:T(8,128)(2,1)S(1)} %bitcast.21, bf16[240,512]{1,0:T(8,128)(2,1)S(1)} %bitcast.19, ...), custom_call_target="tpu_custom_call", output_to_operand_aliasing={{0}: (8, {})} | custom-call | flops 800000000 | bytes 2400000 | tf_op jit(solution)/shard_map/pallas_call | solution.py:299
  10.3 15.1 %collective-permute-start.1 = (bf16[3456,128]{1,0:T(8,128)(2,1)}, bf16[3456,128]{1,0:T(8,128)(2,1)S(1)}, u32[]{:S(2)}, u32[]{:S(2)}) collective-permute-start(bf16[3456,128]{1,0:T(8,128)(2,1)} %get-tuple-element.17), channel_id=1, source_target_pairs={{0,11},{1,0},{2,1},{3,2},{4,3},{5,4},{6,5},{7,6},{8,7},{9,8},{10,9... | collective-permute-start | bytes 2654216 | tf_op jit(solution)/shard_map/ppermute | solution.py:356
  25.5 0.0 copy-done.8
  25.5 2.2 %collective-permute-start.3 = (bf16[1536,128]{1,0:T(8,128)(2,1)S(1)}, bf16[1536,128]{1,0:T(8,128)(2,1)S(1)}, u32[]{:S(2)}, u32[]{:S(2)}) collective-permute-start(bf16[1536,128]{1,0:T(8,128)(2,1)S(1)} %copy-done.8), channel_id=1, source_target_pairs={{0,11},{1,0},{2,1},{3,2},{4,3},{5,4},{6,5},{7,6},{8,7},{9,8},{10,9... | collective-permute-start | bytes 1179656 | tf_op jit(solution)/shard_map/ppermute | solution.py:356
  27.7 2.2 %collective-permute-start = (bf16[240,512]{1,0:T(8,128)(2,1)S(1)}, bf16[240,512]{1,0:T(8,128)(2,1)S(1)}, u32[]{:S(2)}, u32[]{:S(2)}) collective-permute-start(bf16[240,512]{1,0:T(8,128)(2,1)S(1)} %bitcast.22), channel_id=1, source_target_pairs={{0,11},{1,0},{2,1},{3,2},{4,3},{5,4},{6,5},{7,6},{8,7},{9,8},{10,9... | collective-permute-start | bytes 737288 | tf_op jit(solution)/shard_map/ppermute | solution.py:356
  29.9 2.2 %collective-permute-start.2 = (f32[8,8,128]{2,1,0:T(8,128)S(1)}, f32[8,8,128]{2,1,0:T(8,128)}, u32[]{:S(2)}, u32[]{:S(2)}) collective-permute-start(f32[8,8,128]{2,1,0:T(8,128)S(1)} %get-tuple-element.18), channel_id=1, source_target_pairs={{0,11},{1,0},{2,1},{3,2},{4,3},{5,4},{6,5},{7,6},{8,7},{9,8},{10,9... | collective-permute-start | bytes 98312 | tf_op jit(solution)/shard_map/ppermute | solution.py:356
  32.0 26.3 %collective-permute-done.2 = f32[8,8,128]{2,1,0:T(8,128)} collective-permute-done((f32[8,8,128]{2,1,0:T(8,128)S(1)}, f32[8,8,128]{2,1,0:T(8,128)}, u32[]{:S(2)}, u32[]{:S(2)}) %collective-permute-start.2) | collective-permute-done | bytes 32800 | tf_op jit(solution)/shard_map/ppermute | solution.py:356
  58.4 12.4 %all-to-all-start = ((f32[64,1,128]{2,1,0:T(1,128)}), f32[64,1,128]{2,1,0:T(1,128)S(1)}, u32[]{:S(2)}, u32[]{:S(2)}) async-start(f32[64,1,128]{2,1,0:T(1,128)} %bitcast.8), calls=%async_computation | async-start | bytes 65536 | tf_op jit(solution)/shard_map/all_to_all | solution.py:368
  70.8 0.0 collective-permute-done.k_ref
  70.8 0.0 collective-permute-done.3.parcel_ref
  70.8 1.8 %shard_map.112._ = bf16[240,2560]{1,0:T(8,128)(2,1)} custom-call(bf16[240,512]{1,0:T(8,128)(2,1)S(1)} %collective-permute-done.k_ref, bf16[1536,128]{1,0:T(8,128)(2,1)S(1)} %collective-permute-done.3.parcel_ref), custom_call_target="tpu_custom_call" | custom-call | flops 300000000 | bytes 1600000 | tf_op jit(solution)/shard_map/pallas_call | solution.py:322
  72.7 3.4 %all-to-all-done = f32[64,1,128]{2,1,0:T(1,128)S(1)} async-done(((f32[64,1,128]{2,1,0:T(1,128)}), f32[64,1,128]{2,1,0:T(1,128)S(1)}, u32[]{:S(2)}, u32[]{:S(2)}) %all-to-all-start) | async-done | bytes 32800 | tf_op jit(solution)/shard_map/all_to_all | solution.py:368
  76.1 0.0 collective-permute-done.1.parcel_ref
  76.1 2.0 %shard_map.113 = (bf16[240,2560]{1,0:T(8,128)(2,1)}, bf16[240,512]{1,0:T(8,128)(2,1)}, bf16[240,512]{1,0:T(8,128)(2,1)}, f32[1,48]{1,0:T(1,128)}, f32[1,8]{1,0:T(1,128)}) custom-call(bf16[240,512]{1,0:T(8,128)(2,1)S(1)} %collective-permute-done.k_ref, bf16[3456,128]{1,0:T(8,128)(2,1)S(1)} %collective-permute-done.1.parcel_ref, ...), custom_call_target="tpu_custom_call", output_to_operand_aliasing={{0}: (3, {})} | custom-call | flops 300000000 | bytes 2000000 | tf_op jit(solution)/shard_map/pallas_call | solution.py:338
Async XLA Ops:
  0.6 4.9 %copy-start = (bf16[1,240,2560]{2,1,0:T(8,128)(2,1)S(1)}, bf16[1,240,2560]{2,1,0:T(8,128)(2,1)}, u32[]{:S(2)}) copy-start(bf16[1,240,2560]{2,1,0:T(8,128)(2,1)} %param.7) | copy-start | bytes 3686404
  0.6 4.9 %copy-start.1 = (bf16[1,240,2560]{2,1,0:T(8,128)(2,1)S(1)}, bf16[1,240,2560]{2,1,0:T(8,128)(2,1)}, u32[]{:S(2)}) copy-start(bf16[1,240,2560]{2,1,0:T(8,128)(2,1)} %param.10) | copy-start | bytes 3686404
  0.7 4.9 %copy-start.2 = (bf16[1,240,512]{2,1,0:T(8,128)(2,1)S(1)}, bf16[1,240,512]{2,1,0:T(8,128)(2,1)}, u32[]{:S(2)}) copy-start(bf16[1,240,512]{2,1,0:T(8,128)(2,1)} %param.9) | copy-start | bytes 737284
  0.7 4.9 %copy-start.3 = (bf16[1,240,512]{2,1,0:T(8,128)(2,1)S(1)}, bf16[1,240,512]{2,1,0:T(8,128)(2,1)}, u32[]{:S(2)}) copy-start(bf16[1,240,512]{2,1,0:T(8,128)(2,1)} %param.8) | copy-start | bytes 737284
  0.7 4.9 %copy-start.4 = (bf16[1,20,240]{2,1,0:T(8,128)(2,1)S(1)}, bf16[1,20,240]{2,1,0:T(8,128)(2,1)}, u32[]{:S(2)}) copy-start(bf16[1,20,240]{2,1,0:T(8,128)(2,1)} %param.11) | copy-start | bytes 28804
  0.7 4.9 %copy-start.5 = (bf16[1,20,240]{2,1,0:T(8,128)(2,1)S(1)}, bf16[1,20,240]{2,1,0:T(8,128)(2,1)}, u32[]{:S(2)}) copy-start(bf16[1,20,240]{2,1,0:T(8,128)(2,1)} %param.12) | copy-start | bytes 28804
  0.7 4.9 %copy-start.7 = (s32[1,1,3]{2,1,0:T(1,128)S(1)}, s32[1,1,3]{2,1,0:T(1,128)}, u32[]{:S(2)}) copy-start(s32[1,1,3]{2,1,0:T(1,128)} %param.13) | copy-start | bytes 40
  5.6 0.7 copy-start.6
  6.3 19.2 %copy-start.8 = (bf16[1536,128]{1,0:T(8,128)(2,1)S(1)}, bf16[1536,128]{1,0:T(8,128)(2,1)}, u32[]{:S(2)}) copy-start(bf16[1536,128]{1,0:T(8,128)(2,1)} %get-tuple-element.19) | copy-start | bytes 1179652
  10.3 65.8 %collective-permute-start.1 = (bf16[3456,128]{1,0:T(8,128)(2,1)}, bf16[3456,128]{1,0:T(8,128)(2,1)S(1)}, u32[]{:S(2)}, u32[]{:S(2)}) collective-permute-start(bf16[3456,128]{1,0:T(8,128)(2,1)} %get-tuple-element.17), channel_id=1, source_target_pairs={{0,11},{1,0},{2,1},{3,2},{4,3},{5,4},{6,5},{7,6},{8,7},{9,8},{10,9... | collective-permute-start | bytes 2654216 | tf_op jit(solution)/shard_map/ppermute | solution.py:356
  25.5 45.3 %collective-permute-start.3 = (bf16[1536,128]{1,0:T(8,128)(2,1)S(1)}, bf16[1536,128]{1,0:T(8,128)(2,1)S(1)}, u32[]{:S(2)}, u32[]{:S(2)}) collective-permute-start(bf16[1536,128]{1,0:T(8,128)(2,1)S(1)} %copy-done.8), channel_id=1, source_target_pairs={{0,11},{1,0},{2,1},{3,2},{4,3},{5,4},{6,5},{7,6},{8,7},{9,8},{10,9... | collective-permute-start | bytes 1179656 | tf_op jit(solution)/shard_map/ppermute | solution.py:356
  27.7 43.2 %collective-permute-start = (bf16[240,512]{1,0:T(8,128)(2,1)S(1)}, bf16[240,512]{1,0:T(8,128)(2,1)S(1)}, u32[]{:S(2)}, u32[]{:S(2)}) collective-permute-start(bf16[240,512]{1,0:T(8,128)(2,1)S(1)} %bitcast.22), channel_id=1, source_target_pairs={{0,11},{1,0},{2,1},{3,2},{4,3},{5,4},{6,5},{7,6},{8,7},{9,8},{10,9... | collective-permute-start | bytes 737288 | tf_op jit(solution)/shard_map/ppermute | solution.py:356
  29.9 28.5 %collective-permute-start.2 = (f32[8,8,128]{2,1,0:T(8,128)S(1)}, f32[8,8,128]{2,1,0:T(8,128)}, u32[]{:S(2)}, u32[]{:S(2)}) collective-permute-start(f32[8,8,128]{2,1,0:T(8,128)S(1)} %get-tuple-element.18), channel_id=1, source_target_pairs={{0,11},{1,0},{2,1},{3,2},{4,3},{5,4},{6,5},{7,6},{8,7},{9,8},{10,9... | collective-permute-start | bytes 98312 | tf_op jit(solution)/shard_map/ppermute | solution.py:356
  58.4 17.7 %all-to-all-start = ((f32[64,1,128]{2,1,0:T(1,128)}), f32[64,1,128]{2,1,0:T(1,128)S(1)}, u32[]{:S(2)}, u32[]{:S(2)}) async-start(f32[64,1,128]{2,1,0:T(1,128)} %bitcast.8), calls=%async_computation | async-start | bytes 65536 | tf_op jit(solution)/shard_map/all_to_all | solution.py:368
